TPU v7x, 512 devices: a whole 4x4x16 slice. The times are simulated.
512 devices in a mesh: expert: 64 (over z, x_lo, core), hidden: 8 (over x_hi, y).
Axes of the slice: x: 4 (x_hi: 2, x_lo: 2; x = x_hi * 2 + x_lo), y: 4, z: 16, core: 2. Of those that a mesh axis runs over, the one named last changes fastest.
Arguments:
- swap_pairs: int32 [32, 2], replicated, may hold values from 0 to 63, as said below
- expert_ids: int32 [8192, 2], P('expert'), may hold values from 0 to 63, all different within a row; in each aligned block of 128 rows (0 to 127, 128 to 255, ...) at most 8 rows name the same one
- route_weights: float32 [8192, 2], P('expert'), may hold values from 0.05 to 0.6
- gate_up: bfloat16 [8192, 2, 2, 1024], P('expert', None, None, 'hidden'), may hold values from -6 to 6
- grad_out: bfloat16 [8192, 3584], P('expert', 'hidden'), may hold values from -6 to 6
- down_weight: bfloat16 [64, 1024, 3584], P('expert', 'hidden'), may hold values from -0.1875 to 0.1875
- first_moment: bfloat16 [64, 1024, 3584], P('expert', 'hidden'), may hold values from -4 to 4
- second_moment: bfloat16 [64, 1024, 3584], P('expert', 'hidden'), may hold values from 0.049804688 to 1
Outputs:
- combined: bfloat16 [8192, 3584], P('expert', 'hidden')
- grad_gate_up: bfloat16 [8192, 2, 2, 1024], P('expert', None, None, 'hidden')
- adam_step: bfloat16 [64, 1024, 3584], P('expert', 'hidden')
Inputs may be any that keep to these rules, and one draw needn't show every extreme that they name: `swap_pairs`: every place 0 .. 63 appears exactly once in the list. `expert_ids`: A row's 2 experts are distinct; in each aligned block of 128 rows (the rows of one device) no expert is named more than 8 times, a bound that some block reaches.
All inputs are finite; a program needn't handle non-finite values.
Results may differ from a plain program's by a relative error of at most 0.017.
Values may be sent and summed in bfloat16 or wider, within the bound.
A program may use at most 128 MiB of HBM per device.

v0:
```python
import jax
import jax.numpy as jnp
from jax import lax
from jax.sharding import PartitionSpec as P

first_decay = 0.9
second_decay = 0.95
adam_epsilon = 1e-08


def partner_table(swap_pairs, places):
    column = jnp.arange(places, dtype=jnp.int32)
    left = swap_pairs[:, 0]
    right = swap_pairs[:, 1]
    moved = jnp.where(left[:, None] == column[None, :], right[:, None] - column[None, :], 0)
    moved = moved + jnp.where(right[:, None] == column[None, :], left[:, None] - column[None, :], 0)
    return column + jnp.sum(moved, axis=0)


def relocate_state(weight_here, first_here, second_here, partner):
    places = partner.shape[0]
    shape_here = weight_here.shape
    spread = (
        lax.all_to_all(
            weight_here.reshape(places, -1), "expert", split_axis=0, concat_axis=0, tiled=True
        ),
        lax.all_to_all(
            first_here.reshape(places, -1), "expert", split_axis=0, concat_axis=0, tiled=True
        ),
        lax.all_to_all(
            second_here.reshape(places, -1), "expert", split_axis=0, concat_axis=0, tiled=True
        ),
    )
    ordered = tuple((jnp.take(member, partner, axis=0) for member in spread))
    collected = (
        lax.all_to_all(ordered[0], "expert", split_axis=0, concat_axis=0, tiled=True),
        lax.all_to_all(ordered[1], "expert", split_axis=0, concat_axis=0, tiled=True),
        lax.all_to_all(ordered[2], "expert", split_axis=0, concat_axis=0, tiled=True),
    )
    return tuple((member.reshape(shape_here) for member in collected))


def slot_numbers(destination, places, capacity):
    column = jnp.arange(places, dtype=jnp.int32)
    one_hot = (destination[:, None] == column[None, :]).astype(jnp.int32)
    before = jnp.cumsum(one_hot, axis=0) - one_hot
    earlier_count = jnp.sum(before * one_hot, axis=1)
    return destination * capacity + earlier_count


def local(
    swap_pairs,
    expert_ids,
    route_weights,
    gate_up,
    grad_out,
    down_weight,
    first_moment,
    second_moment,
):
    places = lax.axis_size("expert")
    tok_count, top_count = expert_ids.shape
    hid_dev = down_weight.shape[1]
    capacity = 2 * tok_count * top_count // places
    total_slots = places * capacity
    choice_count = tok_count * top_count
    partner = partner_table(swap_pairs, places)
    weight_here = down_weight[0]
    first_here = first_moment[0]
    second_here = second_moment[0]
    flat_ids = expert_ids.reshape(-1)
    column = jnp.arange(places, dtype=jnp.int32)
    weight_here, first_here, second_here = relocate_state(
        weight_here, first_here, second_here, partner
    )
    destination = jnp.sum(
        jnp.where(flat_ids[:, None] == column[None, :], partner[None, :], 0), axis=1
    )
    slot_index = slot_numbers(destination, places, capacity)
    choice_acts = gate_up.reshape(choice_count, 2 * hid_dev)
    scaled = (route_weights[:, :, None] * grad_out[:, None, :].astype(jnp.float32)).astype(
        jnp.bfloat16
    )
    scaled = scaled.reshape(choice_count, grad_out.shape[1])
    send_acts = jnp.zeros((total_slots, 2 * hid_dev), jnp.bfloat16).at[slot_index].set(choice_acts)
    send_grads = (
        jnp.zeros((total_slots, grad_out.shape[1]), jnp.bfloat16).at[slot_index].set(scaled)
    )
    recv_acts, recv_grads = (
        lax.all_to_all(
            send_acts.reshape(places, capacity, 2 * hid_dev),
            "expert",
            split_axis=0,
            concat_axis=0,
            tiled=True,
        ),
        lax.all_to_all(
            send_grads.reshape(places, capacity, grad_out.shape[1]),
            "expert",
            split_axis=0,
            concat_axis=0,
            tiled=True,
        ),
    )
    recv_acts = recv_acts.reshape(total_slots, 2 * hid_dev)
    recv_grads = recv_grads.reshape(total_slots, grad_out.shape[1])
    gate_pre = recv_acts[:, :hid_dev].astype(jnp.float32)
    up_pre = recv_acts[:, hid_dev:].astype(jnp.float32)
    sigmoid_gate = jax.nn.sigmoid(gate_pre)
    silu_gate = gate_pre * sigmoid_gate
    hidden = (silu_gate * up_pre).astype(jnp.bfloat16)
    partial_value = jnp.dot(hidden, weight_here, preferred_element_type=jnp.float32)
    summed = lax.psum_scatter(
        partial_value.astype(jnp.bfloat16), "hidden", scatter_dimension=1, tiled=True
    ).astype(jnp.float32)
    returned = lax.all_to_all(
        summed.reshape(places, capacity, summed.shape[1]).astype(jnp.bfloat16),
        "expert",
        split_axis=0,
        concat_axis=0,
        tiled=True,
    ).astype(jnp.float32)
    per_choice = jnp.take(returned.reshape(total_slots, summed.shape[1]), slot_index, axis=0)
    per_choice = per_choice.reshape(tok_count, top_count, summed.shape[1])
    combined = jnp.einsum("tk,tkd->td", route_weights, per_choice).astype(jnp.bfloat16)
    portion = lax.all_gather(recv_grads, "hidden", axis=1, tiled=True)
    grad_hidden = lax.dot_general(
        portion, weight_here, (((1,), (1,)), ((), ())), preferred_element_type=jnp.float32
    )
    product_block = lax.dot_general(
        hidden, portion, (((0,), (0,)), ((), ())), preferred_element_type=jnp.float32
    )
    grad_weight = product_block
    grad_hidden, grad_weight = (grad_hidden, grad_weight)
    grad_gate = grad_hidden * up_pre * sigmoid_gate * (1.0 + gate_pre * (1.0 - sigmoid_gate))
    grad_up = grad_hidden * silu_gate
    grad_rows = jnp.concatenate([grad_gate, grad_up], axis=1).astype(jnp.bfloat16)
    returned_grads = lax.all_to_all(
        grad_rows.reshape(places, capacity, 2 * hid_dev),
        "expert",
        split_axis=0,
        concat_axis=0,
        tiled=True,
    )
    grad_gate_up = jnp.take(returned_grads.reshape(total_slots, 2 * hid_dev), slot_index, axis=0)
    grad_gate_up = grad_gate_up.reshape(tok_count, top_count, 2, hid_dev)
    first_new = first_decay * first_here.astype(jnp.float32) + (1.0 - first_decay) * grad_weight
    second_new = (
        second_decay * second_here.astype(jnp.float32)
        + (1.0 - second_decay) * grad_weight * grad_weight
    )
    update = (first_new / (jnp.sqrt(second_new) + adam_epsilon)).astype(jnp.bfloat16)
    return (combined, grad_gate_up, update[None])


def solution(mesh):
    placed = (
        P(),
        P("expert", None),
        P("expert", None),
        P("expert", None, None, "hidden"),
        P("expert", "hidden"),
        P("expert", "hidden", None),
        P("expert", "hidden", None),
        P("expert", "hidden", None),
    )
    return jax.shard_map(
        local,
        mesh=mesh,
        in_specs=placed,
        out_specs=(
            P("expert", "hidden"),
            P("expert", None, None, "hidden"),
            P("expert", "hidden", None),
        ),
        check_vma=False,
    )
```

profile of v0, /device:TPU:1, one launch (start us, length us, event | category | flops | bytes accessed | tf_op | source)
XLA Modules:
  0.0 507.0 jit_solution(11949499571279436888)
XLA Ops:
  15.6 18.1 %all-to-all-start.4 = ((bf16[64,8,448]{2,1,0:T(8,128)(2,1)}), bf16[64,8,448]{2,1,0:T(8,128)(2,1)S(1)}, u32[]{:S(2)}, u32[]{:S(2)}) async-start(bf16[64,8,448]{2,1,0:T(8,128)(2,1)} %bitcast.11), calls=%async_computation.5 | async-start | bytes 1048576 | tf_op jit(solution)/shard_map/all_to_all | solution.py:97
  34.7 6.1 %reduce.11 = bf16[64,7168]{1,0:T(8,128)(2,1)S(1)} reduce(bf16[64,1,7168]{2,1,0:T(2,128)(2,1)S(1)} %all_to_all.73, bf16[]{:T(256)} %broadcast.113), dimensions={1}, to_apply=%all_to_all.73.reduce_sub_computation | reduce | bytes 1835010 | tf_op jit(solution)/shard_map/all_to_all | solution.py:24
  42.4 23.7 %all-to-all-done.4 = bf16[64,8,448]{2,1,0:T(8,128)(2,1)S(1)} async-done(((bf16[64,8,448]{2,1,0:T(8,128)(2,1)}), bf16[64,8,448]{2,1,0:T(8,128)(2,1)S(1)}, u32[]{:S(2)}, u32[]{:S(2)}) %all-to-all-start.4) | async-done | bytes 458784 | tf_op jit(solution)/shard_map/all_to_all | solution.py:97
  66.2 7.1 %all-to-all-start.1 = ((bf16[64,2,3584]{2,1,0:T(2,128)(2,1)}), bf16[64,2,3584]{2,1,0:T(2,128)(2,1)}, u32[]{:S(2)}, u32[]{:S(2)}) async-start(bf16[64,2,3584]{2,1,0:T(2,128)(2,1)} %reshape.237), calls=%async_computation.1 | async-start | bytes 1835008 | tf_op jit(solution)/shard_map/all_to_all | solution.py:24
  73.8 6.1 %reduce.10 = bf16[64,7168]{1,0:T(8,128)(2,1)S(1)} reduce(bf16[64,1,7168]{2,1,0:T(2,128)(2,1)S(1)} %all_to_all.75, bf16[]{:T(256)} %broadcast.113), dimensions={1}, to_apply=%all_to_all.75.reduce_sub_computation | reduce | bytes 1835010 | tf_op jit(solution)/shard_map/all_to_all | solution.py:30
  81.6 40.1 %all-to-all-done.1 = bf16[64,2,3584]{2,1,0:T(2,128)(2,1)} async-done(((bf16[64,2,3584]{2,1,0:T(2,128)(2,1)}), bf16[64,2,3584]{2,1,0:T(2,128)(2,1)}, u32[]{:S(2)}, u32[]{:S(2)}) %all-to-all-start.1) | async-done | bytes 917536 | tf_op jit(solution)/shard_map/all_to_all | solution.py:24
  121.7 7.7 %all-to-all-start.8 = ((bf16[64,2,3584]{2,1,0:T(2,128)(2,1)}), bf16[64,2,3584]{2,1,0:T(2,128)(2,1)}, u32[]{:S(2)}, u32[]{:S(2)}) async-start(bf16[64,2,3584]{2,1,0:T(2,128)(2,1)} %reshape.241), calls=%async_computation.9 | async-start | bytes 1835008 | tf_op jit(solution)/shard_map/all_to_all | solution.py:30
  129.9 6.1 %reduce.9 = bf16[64,7168]{1,0:T(8,128)(2,1)S(1)} reduce(bf16[64,1,7168]{2,1,0:T(2,128)(2,1)S(1)} %all_to_all.74, bf16[]{:T(256)} %broadcast.113), dimensions={1}, to_apply=%all_to_all.74.reduce_sub_computation | reduce | bytes 1835010 | tf_op jit(solution)/shard_map/all_to_all | solution.py:27
  137.6 40.1 %all-to-all-done.8 = bf16[64,2,3584]{2,1,0:T(2,128)(2,1)} async-done(((bf16[64,2,3584]{2,1,0:T(2,128)(2,1)}), bf16[64,2,3584]{2,1,0:T(2,128)(2,1)}, u32[]{:S(2)}, u32[]{:S(2)}) %all-to-all-start.8) | async-done | bytes 917536 | tf_op jit(solution)/shard_map/all_to_all | solution.py:30
  177.8 7.3 %all-to-all-start.6 = ((bf16[64,2,3584]{2,1,0:T(2,128)(2,1)}), bf16[64,2,3584]{2,1,0:T(2,128)(2,1)}, u32[]{:S(2)}, u32[]{:S(2)}) async-start(bf16[64,2,3584]{2,1,0:T(2,128)(2,1)} %reshape.245), calls=%async_computation.7 | async-start | bytes 1835008 | tf_op jit(solution)/shard_map/all_to_all | solution.py:27
  188.3 5.4 %reshape.238 = bf16[64,1,7168]{2,1,0:T(2,128)(2,1)S(1)} reshape(bf16[64,2,3584]{2,1,0:T(2,128)(2,1)} %all-to-all-done.1) | data formatting | bytes 1835008
  194.0 6.4 %reshape.242 = bf16[64,1,7168]{2,1,0:T(2,128)(2,1)} reshape(bf16[64,2,3584]{2,1,0:T(2,128)(2,1)} %all-to-all-done.8) | data formatting | bytes 1835008
  206.3 27.4 %all-to-all-done.6 = bf16[64,2,3584]{2,1,0:T(2,128)(2,1)} async-done(((bf16[64,2,3584]{2,1,0:T(2,128)(2,1)}), bf16[64,2,3584]{2,1,0:T(2,128)(2,1)}, u32[]{:S(2)}, u32[]{:S(2)}) %all-to-all-start.6) | async-done | bytes 917536 | tf_op jit(solution)/shard_map/all_to_all | solution.py:27
  233.7 6.9 %all-to-all-start = ((bf16[64,8,256]{2,1,0:T(8,128)(2,1)}), bf16[64,8,256]{2,1,0:T(8,128)(2,1)S(1)}, u32[]{:S(2)}, u32[]{:S(2)}) async-start(bf16[64,8,256]{2,1,0:T(8,128)(2,1)} %bitcast.6), calls=%async_computation | async-start | bytes 524288 | tf_op jit(solution)/shard_map/all_to_all | solution.py:90
  240.6 5.5 %reshape.246 = bf16[64,1,7168]{2,1,0:T(2,128)(2,1)S(1)} reshape(bf16[64,2,3584]{2,1,0:T(2,128)(2,1)} %all-to-all-done.6) | data formatting | bytes 1835008
  255.4 7.6 %all-to-all-done = bf16[64,8,256]{2,1,0:T(8,128)(2,1)S(1)} async-done(((bf16[64,8,256]{2,1,0:T(8,128)(2,1)}), bf16[64,8,256]{2,1,0:T(8,128)(2,1)S(1)}, u32[]{:S(2)}, u32[]{:S(2)}) %all-to-all-start) | async-done | bytes 262176 | tf_op jit(solution)/shard_map/all_to_all | solution.py:90
  262.9 6.1 %all-to-all-start.2 = ((bf16[64,2,3584]{2,1,0:T(2,128)(2,1)}), bf16[64,2,3584]{2,1,0:T(2,128)(2,1)S(1)}, u32[]{:S(2)}, u32[]{:S(2)}) async-start(bf16[64,2,3584]{2,1,0:T(2,128)(2,1)} %reshape.239), calls=%async_computation.2 | async-start | bytes 1835008 | tf_op jit(solution)/shard_map/all_to_all | solution.py:36
  272.0 45.6 %all-to-all-done.2 = bf16[64,2,3584]{2,1,0:T(2,128)(2,1)S(1)} async-done(((bf16[64,2,3584]{2,1,0:T(2,128)(2,1)}), bf16[64,2,3584]{2,1,0:T(2,128)(2,1)S(1)}, u32[]{:S(2)}, u32[]{:S(2)}) %all-to-all-start.2) | async-done | bytes 917536 | tf_op jit(solution)/shard_map/all_to_all | solution.py:36
  317.5 7.3 %all-to-all-start.7 = ((bf16[64,2,3584]{2,1,0:T(2,128)(2,1)}), bf16[64,2,3584]{2,1,0:T(2,128)(2,1)}, u32[]{:S(2)}, u32[]{:S(2)}) async-start(bf16[64,2,3584]{2,1,0:T(2,128)(2,1)} %reshape.247), calls=%async_computation.8 | async-start | bytes 1835008 | tf_op jit(solution)/shard_map/all_to_all | solution.py:37
  325.7 5.5 %reduce.2 = bf16[64,7168]{1,0:T(8,128)(2,1)S(1)} reduce(bf16[64,1,7168]{2,1,0:T(2,128)(2,1)S(1)} %reshape.240, bf16[]{:T(256)} %constant.68), dimensions={1}, to_apply=%all_to_all.59.reduce_sub_computation | reduce | bytes 1835010 | tf_op jit(solution)/shard_map/all_to_all | solution.py:36
  331.6 3.0 convolution_convert_fusion
  338.7 34.8 %all-to-all-done.7 = bf16[64,2,3584]{2,1,0:T(2,128)(2,1)} async-done(((bf16[64,2,3584]{2,1,0:T(2,128)(2,1)}), bf16[64,2,3584]{2,1,0:T(2,128)(2,1)}, u32[]{:S(2)}, u32[]{:S(2)}) %all-to-all-start.7) | async-done | bytes 917536 | tf_op jit(solution)/shard_map/all_to_all | solution.py:37
  373.5 6.6 %all-to-all-start.9 = ((bf16[64,2,3584]{2,1,0:T(2,128)(2,1)}), bf16[64,2,3584]{2,1,0:T(2,128)(2,1)S(1)}, u32[]{:S(2)}, u32[]{:S(2)}) async-start(bf16[64,2,3584]{2,1,0:T(2,128)(2,1)} %reshape.243), calls=%async_computation.10 | async-start | bytes 1835008 | tf_op jit(solution)/shard_map/all_to_all | solution.py:38
  380.1 3.3 fusion.22
  384.1 44.6 %all-to-all-done.9 = bf16[64,2,3584]{2,1,0:T(2,128)(2,1)S(1)} async-done(((bf16[64,2,3584]{2,1,0:T(2,128)(2,1)}), bf16[64,2,3584]{2,1,0:T(2,128)(2,1)S(1)}, u32[]{:S(2)}, u32[]{:S(2)}) %all-to-all-start.9) | async-done | bytes 917536 | tf_op jit(solution)/shard_map/all_to_all | solution.py:38
  428.7 6.8 %all-to-all-start.5 = ((bf16[64,8,256]{2,1,0:T(8,128)(2,1)}), bf16[64,8,256]{2,1,0:T(8,128)(2,1)S(1)}, u32[]{:S(2)}, u32[]{:S(2)}) async-start(bf16[64,8,256]{2,1,0:T(8,128)(2,1)} %pad_maximum_fusion), calls=%async_computation.6 | async-start | bytes 524288 | tf_op jit(solution)/shard_map/all_to_all | solution.py:138
  438.7 18.9 %all-to-all-done.5 = bf16[64,8,256]{2,1,0:T(8,128)(2,1)S(1)} async-done(((bf16[64,8,256]{2,1,0:T(8,128)(2,1)}), bf16[64,8,256]{2,1,0:T(8,128)(2,1)S(1)}, u32[]{:S(2)}, u32[]{:S(2)}) %all-to-all-start.5) | async-done | bytes 262176 | tf_op jit(solution)/shard_map/all_to_all | solution.py:138
  457.7 4.7 all-to-all-start.3
  463.0 6.4 %reshape.248 = bf16[64,1,7168]{2,1,0:T(2,128)(2,1)} reshape(bf16[64,2,3584]{2,1,0:T(2,128)(2,1)} %all-to-all-done.7) | data formatting | bytes 1835008
  469.4 7.1 %multiply_reduce_fusion.1 = f32[64,7168]{1,0:T(8,128)S(1)} fusion(bf16[64,1,7168]{2,1,0:T(2,128)(2,1)} %reshape.248), kind=kLoop, calls=%fused_computation.14 | loop fusion | flops 917504 | bytes 2752512 | tf_op jit(solution)/shard_map/mul | solution.py:147
  480.4 7.1 %multiply_reduce_fusion = f32[64,7168]{1,0:T(8,128)S(1)} fusion(bf16[64,1,7168]{2,1,0:T(2,128)(2,1)} %reshape.244), kind=kLoop, calls=%fused_computation.13 | loop fusion | flops 917504 | bytes 2752512 | tf_op jit(solution)/shard_map/mul | solution.py:149
  489.1 5.6 %fusion.5 = bf16[1,128,3584]{2,1,0:T(8,128)(2,1)} fusion(f32[128,3584]{1,0:T(8,128)} %mul.115, f32[128,3584]{1,0:T(8,128)} %mul.110, bf16[512,3584]{0,1:T(8,128)(2,1)} %all-gather.2.cloned.1.call-done, bf16[512,256]{1,0:T(8,128)(2,1)S(1)} %bitcast.72), kind=kOutput, calls=%fused_computation.22 | convolution fusion | flops 473956352 | bytes 8519680 | tf_op jit(solution)/shard_map/dot_general | solution.py:130
  (99 shorter events, 57.2 us)
Async XLA Ops:
  10.0 176.1 %copy-start.13 = (s32[256,1]{0,1:T(1,128)}, s32[256,1]{0,1:T(1,128)S(1)}, u32[]{:S(2)}) copy-start(s32[256,1]{0,1:T(1,128)S(1)} %compare_select_fusion.1) | copy-start | bytes 3076
  10.8 0.6 copy-start.9
  12.6 21.0 %copy-start.4 = (bf16[1,128,3584]{2,1,0:T(8,128)(2,1)S(1)}, bf16[1,128,3584]{2,1,0:T(8,128)(2,1)}, u32[]{:S(2)}) copy-start(bf16[1,128,3584]{2,1,0:T(8,128)(2,1)} %param.15) | copy-start | bytes 2752516
  15.6 50.6 %all-to-all-start.4 = ((bf16[64,8,448]{2,1,0:T(8,128)(2,1)}), bf16[64,8,448]{2,1,0:T(8,128)(2,1)S(1)}, u32[]{:S(2)}, u32[]{:S(2)}) async-start(bf16[64,8,448]{2,1,0:T(8,128)(2,1)} %bitcast.11), calls=%async_computation.5 | async-start | bytes 1048576 | tf_op jit(solution)/shard_map/all_to_all | solution.py:97
  42.4 30.9 %copy-start.5 = (bf16[1,128,3584]{2,1,0:T(8,128)(2,1)S(1)}, bf16[1,128,3584]{2,1,0:T(8,128)(2,1)}, u32[]{:S(2)}) copy-start(bf16[1,128,3584]{2,1,0:T(8,128)(2,1)} %param.17) | copy-start | bytes 2752516
  66.2 55.5 %all-to-all-start.1 = ((bf16[64,2,3584]{2,1,0:T(2,128)(2,1)}), bf16[64,2,3584]{2,1,0:T(2,128)(2,1)}, u32[]{:S(2)}, u32[]{:S(2)}) async-start(bf16[64,2,3584]{2,1,0:T(2,128)(2,1)} %reshape.237), calls=%async_computation.1 | async-start | bytes 1835008 | tf_op jit(solution)/shard_map/all_to_all | solution.py:24
  81.6 47.8 %copy-start.6 = (bf16[1,128,3584]{2,1,0:T(8,128)(2,1)S(1)}, bf16[1,128,3584]{2,1,0:T(8,128)(2,1)}, u32[]{:S(2)}) copy-start(bf16[1,128,3584]{2,1,0:T(8,128)(2,1)} %param.16) | copy-start | bytes 2752516
  121.7 56.1 %all-to-all-start.8 = ((bf16[64,2,3584]{2,1,0:T(2,128)(2,1)}), bf16[64,2,3584]{2,1,0:T(2,128)(2,1)}, u32[]{:S(2)}, u32[]{:S(2)}) async-start(bf16[64,2,3584]{2,1,0:T(2,128)(2,1)} %reshape.241), calls=%async_computation.9 | async-start | bytes 1835008 | tf_op jit(solution)/shard_map/all_to_all | solution.py:30
  137.6 48.5 %copy-start.11 = (bf16[128,2,2,128]{3,2,1,0:T(2,128)(2,1)S(1)}, bf16[128,2,2,128]{3,2,1,0:T(2,128)(2,1)}, u32[]{:S(2)}) copy-start(bf16[128,2,2,128]{3,2,1,0:T(2,128)(2,1)} %param.13) | copy-start | bytes 393220
  177.8 55.9 %all-to-all-start.6 = ((bf16[64,2,3584]{2,1,0:T(2,128)(2,1)}), bf16[64,2,3584]{2,1,0:T(2,128)(2,1)}, u32[]{:S(2)}, u32[]{:S(2)}) async-start(bf16[64,2,3584]{2,1,0:T(2,128)(2,1)} %reshape.245), calls=%async_computation.7 | async-start | bytes 1835008 | tf_op jit(solution)/shard_map/all_to_all | solution.py:27
  185.1 195.0 %all-gather.2.cloned.1.call-start = ((), (), s32[]{:S(2)}) async-start(), calls=%async_computation.12 | async-start | bytes 4128768 | tf_op jit(solution)/shard_map/all_gather | solution.py:126
  233.7 29.3 %all-to-all-start = ((bf16[64,8,256]{2,1,0:T(8,128)(2,1)}), bf16[64,8,256]{2,1,0:T(8,128)(2,1)S(1)}, u32[]{:S(2)}, u32[]{:S(2)}) async-start(bf16[64,8,256]{2,1,0:T(8,128)(2,1)} %bitcast.6), calls=%async_computation | async-start | bytes 524288 | tf_op jit(solution)/shard_map/all_to_all | solution.py:90
  246.4 2.1 copy-start
  246.4 2.1 copy-start.1
  253.8 15.3 %copy-start.3 = (bf16[64,1,7168]{2,0,1:T(8,128)(2,1)S(1)}, bf16[64,1,7168]{2,0,1:T(8,128)(2,1)}, u32[]{:S(2)}) copy-start(bf16[64,1,7168]{2,0,1:T(8,128)(2,1)} %get-tuple-element.10) | copy-start | bytes 2752516
  262.9 117.1 %copy-start.7 = (bf16[64,8,256]{2,1,0:T(8,128)(2,1)}, bf16[64,8,256]{2,1,0:T(8,128)(2,1)S(1)}, u32[]{:S(2)}) copy-start(bf16[64,8,256]{2,1,0:T(8,128)(2,1)S(1)} %all-to-all-done) | copy-start | bytes 786436
  262.9 54.6 %all-to-all-start.2 = ((bf16[64,2,3584]{2,1,0:T(2,128)(2,1)}), bf16[64,2,3584]{2,1,0:T(2,128)(2,1)S(1)}, u32[]{:S(2)}, u32[]{:S(2)}) async-start(bf16[64,2,3584]{2,1,0:T(2,128)(2,1)} %reshape.239), calls=%async_computation.2 | async-start | bytes 1835008 | tf_op jit(solution)/shard_map/all_to_all | solution.py:36
  317.5 55.9 %all-to-all-start.7 = ((bf16[64,2,3584]{2,1,0:T(2,128)(2,1)}), bf16[64,2,3584]{2,1,0:T(2,128)(2,1)}, u32[]{:S(2)}, u32[]{:S(2)}) async-start(bf16[64,2,3584]{2,1,0:T(2,128)(2,1)} %reshape.247), calls=%async_computation.8 | async-start | bytes 1835008 | tf_op jit(solution)/shard_map/all_to_all | solution.py:37
  324.9 111.8 %reduce-scatter.2.cloned.1.call-start = ((), (), s32[]{:S(2)}) async-start(), calls=%async_computation.11 | async-start | bytes 4128768 | tf_op jit(solution)/shard_map/reduce_scatter | solution.py:113
  334.6 1.2 copy-start.2
  373.5 55.2 %all-to-all-start.9 = ((bf16[64,2,3584]{2,1,0:T(2,128)(2,1)}), bf16[64,2,3584]{2,1,0:T(2,128)(2,1)S(1)}, u32[]{:S(2)}, u32[]{:S(2)}) async-start(bf16[64,2,3584]{2,1,0:T(2,128)(2,1)} %reshape.243), calls=%async_computation.10 | async-start | bytes 1835008 | tf_op jit(solution)/shard_map/all_to_all | solution.py:38
  383.3 79.1 %copy-start.14 = (s32[256,1]{0,1:T(1,128)S(1)}, s32[256,1]{0,1:T(1,128)}, u32[]{:S(2)}) copy-start(s32[256,1]{0,1:T(1,128)} %copy-done.13) | copy-start | bytes 3076
  428.7 29.0 %all-to-all-start.5 = ((bf16[64,8,256]{2,1,0:T(8,128)(2,1)}), bf16[64,8,256]{2,1,0:T(8,128)(2,1)S(1)}, u32[]{:S(2)}, u32[]{:S(2)}) async-start(bf16[64,8,256]{2,1,0:T(8,128)(2,1)} %pad_maximum_fusion), calls=%async_computation.6 | async-start | bytes 524288 | tf_op jit(solution)/shard_map/all_to_all | solution.py:138
  457.7 39.2 %all-to-all-start.3 = ((bf16[64,8,448]{2,1,0:T(8,128)(2,1)}), bf16[64,8,448]{2,1,0:T(8,128)(2,1)S(1)}, u32[]{:S(2)}, u32[]{:S(2)}) async-start(bf16[64,8,448]{2,1,0:T(8,128)(2,1)} %bitcast.9), calls=%async_computation.4 | async-start | bytes 1048576 | tf_op jit(solution)/shard_map/all_to_all | solution.py:116
  487.5 1.6 copy-start.8
  489.0 5.6 %copy-start.12 = (s32[1024]{0:T(1024)S(1)}, s32[1024]{0:T(1024)}, u32[]{:S(2)}) copy-start(s32[1024]{0:T(1024)} %pad_clamp_fusion) | copy-start | bytes 12292
  497.0 1.3 copy-start.10
Sparse Core Ops, SparseCore 0:
  189.1 86.6 all-gather.1
  334.7 101.9 reduce-scatter.1
where the time goes:
time: 517 us; the launch traced here: 507 us
  waiting for transfers between devices  284 us (55%)
  starting transfers between devices  78.8 us (15%)
  local copies, waits for them, and re-layouts  65 us (13%)
  other arithmetic  52.7 us (10%)
  between operations  14.7 us (3%)
  matrix products  11.9 us (2%)
    all_to_all x1, waiting for transfers between devices, relocate_state(): lax.all_to_all(ordered[0], 'expert', split_axis=0, concat_axis=0, tiled=T...  45.6 us
    all_to_all x1, waiting for transfers between devices, relocate_state(): lax.all_to_all(ordered[2], 'expert', split_axis=0, concat_axis=0, tiled=T...  44.6 us
    unnamed x47, local copies, waits for them, and re-layouts  42 us
    all_to_all x1, waiting for transfers between devices, relocate_state(): lax.all_to_all(second_here.reshape(places, -1), 'expert', split_axis=0, c...  40.1 us
    all_to_all x1, waiting for transfers between devices, relocate_state(): lax.all_to_all(weight_here.reshape(places, -1), 'expert', split_axis=0, c...  40.1 us
    all_to_all x1, waiting for transfers between devices, relocate_state(): lax.all_to_all(ordered[1], 'expert', split_axis=0, concat_axis=0, tiled=T...  34.8 us
    all_to_all x1, waiting for transfers between devices, relocate_state(): lax.all_to_all(first_here.reshape(places, -1), 'expert', split_axis=0, co...  27.4 us
    all_to_all x1, waiting for transfers between devices, local(): lax.all_to_all(send_grads.reshape(places, capacity, grad_out.shape[1]), '...  23.7 us
  transfers between devices with their start and end apart: 12, of which 10 were waited for; matrix products, arithmetic and copies ran while one was open for 23% of the time, Pallas kernels for 0%

commit v1 on v0

v1 whole, which is shorter than its diff:
```python
import functools

import jax
import jax.numpy as jnp
from jax import lax
from jax.experimental import pallas as pl
from jax.experimental.pallas import tpu as pltpu
from jax.sharding import PartitionSpec as P

first_decay = 0.9
second_decay = 0.95
adam_epsilon = 1e-08
ROWS = 16
COLS = 512


def partner_table(swap_pairs, places):
    column = jnp.arange(places, dtype=jnp.int32)
    left = swap_pairs[:, 0]
    right = swap_pairs[:, 1]
    moved = jnp.where(left[:, None] == column[None, :], right[:, None] - column[None, :], 0)
    moved = moved + jnp.where(right[:, None] == column[None, :], left[:, None] - column[None, :], 0)
    return column + jnp.sum(moved, axis=0)


def dot(a, b, contract_a, contract_b):
    return lax.dot_general(
        a, b, (((contract_a,), (contract_b,)), ((), ())), preferred_element_type=jnp.float32
    )


def kernel(
    places,
    n_hidden,
    capacity,
    partner_ref,
    ids_ref,
    route_ref,
    acts_ref,
    gout_ref,
    w_hbm,
    m_hbm,
    v_hbm,
    comb_ref,
    ggu_ref,
    upd_hbm,
    w_here,
    m_here,
    v_here,
    table,
    h_send,
    h_recv,
    g_send,
    g_recv,
    w_send,
    w_recv,
    h_own,
    h_all,
    y_send,
    y_recv,
    gw_send,
    gw_recv,
    gh_send,
    gh_recv,
    gr_send,
    gr_recv,
    u_here,
    u_mid,
    u_out,
    u_new,
    local_sem,
    send_sem,
    recv_sem,
):
    me = lax.axis_index("expert")
    mine = lax.axis_index("hidden")
    tok = ids_ref.shape[0]
    slots = places * capacity
    unit = h_own.shape[1]
    feat = gout_ref.shape[1]
    col_groups = w_here.shape[1] // COLS
    row_groups = w_here.shape[0] // ROWS
    stride = places // row_groups

    def expert_peer(step):
        half = (step + 1) // 2
        return lax.rem(me + half + (1 - lax.rem(step, 2)) * (places - 2 * half), places)

    def hidden_peer(step):
        return lax.rem(mine + step, n_hidden)

    barrier = pltpu.get_barrier_semaphore()

    def greet_expert(step, carry):
        pl.semaphore_signal(barrier, inc=1, device_id={"expert": lax.rem(me + step, places)})
        return carry

    def greet_hidden(step, carry):
        pl.semaphore_signal(barrier, inc=1, device_id={"hidden": hidden_peer(step)})
        return carry

    lax.fori_loop(1, places, greet_expert, 0)
    lax.fori_loop(1, n_hidden, greet_hidden, 0)

    loads = [
        pltpu.make_async_copy(src, dst, local_sem.at[at])
        for at, (src, dst) in enumerate(((w_hbm, w_here), (m_hbm, m_here), (v_hbm, v_here)))
    ]
    for load in loads:
        load.start()

    ids = jnp.concatenate([ids_ref[:, 0:1], ids_ref[:, 1:2]], axis=0)
    count = 2 * tok
    hot = (ids == lax.broadcasted_iota(jnp.int32, (count, 128), 1)).astype(jnp.float32)
    earlier = (
        lax.broadcasted_iota(jnp.int32, (count, count), 1)
        < lax.broadcasted_iota(jnp.int32, (count, count), 0)
    ).astype(jnp.bfloat16)
    before = dot(earlier, hot.astype(jnp.bfloat16), 1, 0)
    rank = jnp.sum(before * hot, axis=1, keepdims=True).astype(jnp.int32)
    slot = ids * capacity + rank
    table[...] = (slot == lax.broadcasted_iota(jnp.int32, (count, slots), 1)).astype(jnp.bfloat16)

    def gate_and_up(choice):
        at = choice * 2 * unit
        gate = acts_ref[:, at : at + unit].astype(jnp.float32)
        up = acts_ref[:, at + unit : at + 2 * unit].astype(jnp.float32)
        return gate, up

    rows = []
    for choice in range(2):
        gate, up = gate_and_up(choice)
        rows.append((gate * jax.nn.sigmoid(gate) * up).astype(jnp.bfloat16))
    placed = dot(table[...], jnp.concatenate(rows, axis=0), 0, 0)
    h_send[...] = placed.reshape(places, capacity, unit).astype(jnp.bfloat16)

    def to_experts(src, dst, at):
        def send(step, carry):
            peer = expert_peer(step)
            pltpu.make_async_remote_copy(
                src_ref=src.at[peer],
                dst_ref=dst.at[me],
                send_sem=send_sem.at[at],
                recv_sem=recv_sem.at[at],
                device_id={"expert": peer},
            ).start()
            return carry

        lax.fori_loop(1, places, send, 0)
        pltpu.make_async_copy(src.at[me], dst.at[me], recv_sem.at[at]).start()

    def to_hidden(src, dst, at, block=True):
        def send(step, carry):
            peer = hidden_peer(step)
            pltpu.make_async_remote_copy(
                src_ref=src.at[peer] if block else src,
                dst_ref=dst.at[mine],
                send_sem=send_sem.at[at],
                recv_sem=recv_sem.at[at],
                device_id={"hidden": peer},
            ).start()
            return carry

        lax.fori_loop(1, n_hidden, send, 0)
        pltpu.make_async_copy(
            src.at[mine] if block else src, dst.at[mine], recv_sem.at[at]
        ).start()

    def arrived(dst, at):
        pltpu.make_async_copy(dst, dst, recv_sem.at[at]).wait()

    def sent(src, at):
        pltpu.make_async_copy(src, src, send_sem.at[at]).wait()

    pl.semaphore_wait(barrier, places + n_hidden - 2)
    to_experts(h_send, h_recv, 0)

    loads[0].wait()
    for block in range(n_hidden):
        w_send[block] = w_here[:, block * feat : (block + 1) * feat]
    to_hidden(w_send, w_recv, 1)

    rows = [
        (route_ref[:, choice : choice + 1] * gout_ref[...].astype(jnp.float32)).astype(jnp.bfloat16)
        for choice in range(2)
    ]
    placed = dot(table[...], jnp.concatenate(rows, axis=0), 0, 0)
    g_send[...] = placed.reshape(places, capacity, feat).astype(jnp.bfloat16)
    to_experts(g_send, g_recv, 2)

    arrived(h_recv, 0)
    h_own[...] = h_recv[...].astype(jnp.float32).reshape(slots, unit).astype(jnp.bfloat16)
    to_hidden(h_own, h_all, 3, block=False)

    arrived(h_all, 3)
    arrived(w_recv, 1)
    w_all = w_recv[...].reshape(n_hidden * unit, feat)
    h_cat = jnp.concatenate([h_all[block] for block in range(n_hidden)], axis=1)
    y_send[...] = dot(h_cat, w_all, 1, 0).reshape(places, capacity, feat).astype(jnp.bfloat16)
    to_experts(y_send, y_recv, 4)

    arrived(g_recv, 2)
    grads = g_recv[...].astype(jnp.float32).reshape(slots, feat).astype(jnp.bfloat16)
    for block in range(n_hidden):
        gw_send[block] = dot(h_all[block], grads, 0, 0).astype(jnp.bfloat16)
    to_hidden(gw_send, gw_recv, 5)
    for block in range(n_hidden):
        gh_send[block] = dot(grads, w_recv[block], 1, 1).astype(jnp.bfloat16)
    to_hidden(gh_send, gh_recv, 6)

    arrived(gw_recv, 5)
    loads[1].wait()
    loads[2].wait()
    is_mid = lax.rem(me, stride) < col_groups
    my_row = pl.multiple_of((me // stride) * ROWS, ROWS)
    my_col = pl.multiple_of(lax.rem(me, stride) * COLS, COLS)

    def update_rows(step, carry):
        half = (step + 1) // 2
        group = lax.rem(
            me // stride + half + (1 - lax.rem(step, 2)) * (row_groups - 2 * half), row_groups
        )
        at = pl.multiple_of(group * ROWS, ROWS)
        for pair in range(n_hidden // 2):
            span = slice(pair * 2 * feat, (pair + 1) * 2 * feat)
            grad = jnp.concatenate(
                [
                    gw_recv[2 * pair, pl.ds(at, ROWS), :],
                    gw_recv[2 * pair + 1, pl.ds(at, ROWS), :],
                ],
                axis=1,
            ).astype(jnp.float32)
            first = m_here[pl.ds(at, ROWS), span].astype(jnp.float32)
            second = v_here[pl.ds(at, ROWS), span].astype(jnp.float32)
            first_new = first_decay * first + (1.0 - first_decay) * grad
            second_new = second_decay * second + (1.0 - second_decay) * grad * grad
            u_here[pl.ds(at, ROWS), span] = (
                first_new / (jnp.sqrt(second_new) + adam_epsilon)
            ).astype(jnp.bfloat16)

        def send(col, carry):
            peer = group * stride + col
            chunk = u_here.at[pl.ds(at, ROWS), pl.ds(pl.multiple_of(col * COLS, COLS), COLS)]

            @pl.when(peer == me)
            def _():
                pltpu.make_async_copy(chunk, u_mid.at[me], recv_sem.at[7]).start()

            @pl.when(peer != me)
            def _():
                pltpu.make_async_remote_copy(
                    src_ref=chunk,
                    dst_ref=u_mid.at[me],
                    send_sem=send_sem.at[7],
                    recv_sem=recv_sem.at[7],
                    device_id={"expert": peer},
                ).start()

            return carry

        return lax.fori_loop(0, col_groups, send, carry)

    lax.fori_loop(0, row_groups, update_rows, 0)

    arrived(gh_recv, 6)
    total = gh_recv[0].astype(jnp.float32)
    for block in range(1, n_hidden):
        total = total + gh_recv[block].astype(jnp.float32)
    gr_send[...] = total.reshape(places, capacity, unit).astype(jnp.bfloat16)
    to_experts(gr_send, gr_recv, 8)

    arrived(y_recv, 4)
    back = y_recv[...].astype(jnp.float32).reshape(slots, feat).astype(jnp.bfloat16)
    picked = dot(table[...], back, 1, 0)
    comb_ref[...] = (
        route_ref[:, 0:1] * picked[:tok] + route_ref[:, 1:2] * picked[tok:]
    ).astype(jnp.bfloat16)

    @pl.when(is_mid)
    def _():
        arrived(u_mid, 7)

        def forward(step, carry):
            peer = expert_peer(step)
            u_out[peer] = u_mid[partner_ref[peer]]
            pltpu.make_async_remote_copy(
                src_ref=u_out.at[peer],
                dst_ref=u_new.at[pl.ds(my_row, ROWS), pl.ds(my_col, COLS)],
                send_sem=send_sem.at[9],
                recv_sem=recv_sem.at[9],
                device_id={"expert": peer},
            ).start()
            return carry

        lax.fori_loop(1, places, forward, 0)
        u_out[me] = u_mid[partner_ref[me]]
        pltpu.make_async_copy(
            u_out.at[me], u_new.at[pl.ds(my_row, ROWS), pl.ds(my_col, COLS)], recv_sem.at[9]
        ).start()

    arrived(gr_recv, 8)
    back = gr_recv[...].astype(jnp.float32).reshape(slots, unit).astype(jnp.bfloat16)
    picked = dot(table[...], back, 1, 0)
    for choice in range(2):
        gate, up = gate_and_up(choice)
        sig = jax.nn.sigmoid(gate)
        grad_hidden = picked[choice * tok : (choice + 1) * tok]
        at = choice * 2 * unit
        ggu_ref[:, at : at + unit] = (
            grad_hidden * up * sig * (1.0 + gate * (1.0 - sig))
        ).astype(jnp.bfloat16)
        ggu_ref[:, at + unit : at + 2 * unit] = (grad_hidden * (gate * sig)).astype(jnp.bfloat16)

    arrived(u_new, 9)
    store = pltpu.make_async_copy(u_new, upd_hbm, local_sem.at[0])
    store.start()
    for at, src in ((0, h_send), (2, g_send), (4, y_send), (8, gr_send)):
        sent(src.at[pl.ds(0, places - 1)], at)
    for at, src in ((1, w_send), (3, h_all), (5, gw_send), (6, gh_send)):
        sent(src.at[pl.ds(0, n_hidden - 1)], at)

    @pl.when(is_mid)
    def _():
        sent(u_mid.at[pl.ds(0, row_groups * col_groups - 1)], 7)
        sent(u_out.at[pl.ds(0, places - 1)], 9)

    @pl.when(jnp.logical_not(is_mid))
    def _():
        sent(u_mid.at[pl.ds(0, row_groups * col_groups)], 7)

    store.wait()


def local(
    swap_pairs,
    expert_ids,
    route_weights,
    gate_up,
    grad_out,
    down_weight,
    first_moment,
    second_moment,
):
    places = lax.axis_size("expert")
    n_hidden = lax.axis_size("hidden")
    tok, top = expert_ids.shape
    unit, depth = down_weight.shape[1:]
    feat = grad_out.shape[1]
    capacity = 2 * tok * top // places
    slots = places * capacity
    partner = partner_table(swap_pairs, places)
    bf16 = jnp.bfloat16
    vmem = pl.BlockSpec(memory_space=pltpu.VMEM)
    anywhere = pl.BlockSpec(memory_space=pl.ANY)
    scratch = [
        ((unit, depth), bf16),
        ((unit, depth), bf16),
        ((unit, depth), bf16),
        ((tok * top, slots), bf16),
        ((places, capacity, unit), bf16),
        ((places, capacity, unit), bf16),
        ((places, capacity, feat), bf16),
        ((places, capacity, feat), bf16),
        ((n_hidden, unit, feat), bf16),
        ((n_hidden, unit, feat), bf16),
        ((slots, unit), bf16),
        ((n_hidden, slots, unit), bf16),
        ((places, capacity, feat), bf16),
        ((places, capacity, feat), bf16),
        ((n_hidden, unit, feat), bf16),
        ((n_hidden, unit, feat), bf16),
        ((n_hidden, slots, unit), bf16),
        ((n_hidden, slots, unit), bf16),
        ((places, capacity, unit), bf16),
        ((places, capacity, unit), bf16),
        ((unit, depth), bf16),
        ((places, ROWS, COLS), bf16),
        ((places, ROWS, COLS), bf16),
        ((unit, depth), bf16),
    ]
    combined, grads, update = pl.pallas_call(
        functools.partial(kernel, places, n_hidden, capacity),
        out_shape=(
            jax.ShapeDtypeStruct((tok, feat), bf16),
            jax.ShapeDtypeStruct((tok, top * 2 * unit), bf16),
            jax.ShapeDtypeStruct((unit, depth), bf16),
        ),
        in_specs=[pl.BlockSpec(memory_space=pltpu.SMEM)] + [vmem] * 4 + [anywhere] * 3,
        out_specs=(vmem, vmem, anywhere),
        scratch_shapes=[pltpu.VMEM(shape, kind) for shape, kind in scratch]
        + [
            pltpu.SemaphoreType.DMA((3,)),
            pltpu.SemaphoreType.DMA((10,)),
            pltpu.SemaphoreType.DMA((10,)),
        ],
        compiler_params=pltpu.CompilerParams(
            collective_id=0, has_side_effects=True, vmem_limit_bytes=48 * 1024 * 1024
        ),
    )(
        partner,
        expert_ids,
        route_weights,
        gate_up.reshape(tok, top * 2 * unit),
        grad_out,
        down_weight[0],
        first_moment[0],
        second_moment[0],
    )
    return combined, grads.reshape(tok, top, 2, unit), update[None]


def solution(mesh):
    placed = (
        P(),
        P("expert", None),
        P("expert", None),
        P("expert", None, None, "hidden"),
        P("expert", "hidden"),
        P("expert", "hidden", None),
        P("expert", "hidden", None),
        P("expert", "hidden", None),
    )
    return jax.shard_map(
        local,
        mesh=mesh,
        in_specs=placed,
        out_specs=(
            P("expert", "hidden"),
            P("expert", None, None, "hidden"),
            P("expert", "hidden", None),
        ),
        check_vma=False,
    )
```

time: 517 us -> 183 us (0.35)
  the two profiles are of different devices: /device:TPU:1 before, /device:TPU:24 now
where the time goes in v1:
time: 183 us; the launch traced here: 182 us
  Pallas kernels  172 us (94%)
  local copies, waits for them, and re-layouts  9.24 us (5%)
    pallas_call x1, Pallas kernels, local(): pl.pallas_call(functools.partial(kernel, places, n_hidden, capacity), out...  172 us
    unnamed x15, local copies, waits for them, and re-layouts  7.74 us

profile of v1, /device:TPU:24, one launch (start us, length us, event | category | flops | bytes accessed | tf_op | source)
XLA Modules:
  0.0 182.5 jit_solution(10280701231107706500)
XLA Ops:
  0.6 0.0 copy-start.3
  0.6 0.8 slice_bitcast_fusion.1
  1.4 0.1 add_reduce_fusion
  1.5 0.8 copy.15.ids_ref
  2.3 0.8 copy.16.route_ref
  3.1 0.0 copy-done.3
  3.1 0.0 copy-start.4
  3.1 0.1 reshape.12.acts_ref
  3.1 0.8 copy-done.4
  4.0 0.1 copy.17.gout_ref
  4.1 0.0 copy-start
  4.1 1.2 copy-done
  5.3 0.0 copy-start.1
  5.3 1.2 copy-done.1
  6.5 0.0 copy-start.2
  6.5 1.2 copy-done.2
  7.6 172.5 %shard_map.103 = (bf16[128,448]{1,0:T(8,128)(2,1)S(1)}, bf16[128,512]{1,0:T(8,128)(2,1)S(1)}, bf16[128,3584]{1,0:T(8,128)(2,1)S(1)}) custom-call(s32[64]{0:T(128)S(1)} %iota_add_fusion.partner_ref, s32[128,2]{1,0:T(8,128)S(1)} %copy.15.ids_ref, f32[128,2]{1,0:T(8,128)S(1)} %copy.16.route_ref, bf16[128,512]{1,0:T(8,128)(2,1)S(1)} %reshape.12.acts_ref, ...), custom_call_target="tpu_custom_call" | custom-call | tf_op jit(solution)/shard_map/pallas_call | solution.py:381
  180.1 0.8 copy.18
  180.9 0.7 reshape.13
  181.6 0.9 copy.20
  (1 shorter events, 0.0 us)
Async XLA Ops:
  0.6 2.4 %copy-start.3 = (bf16[128,2,2,128]{3,2,1,0:T(2,128)(2,1)S(1)}, bf16[128,2,2,128]{3,2,1,0:T(2,128)(2,1)}, u32[]{:S(2)}) copy-start(bf16[128,2,2,128]{3,2,1,0:T(2,128)(2,1)} %param.11) | copy-start | bytes 393220
  3.1 0.9 copy-start.4
  4.1 1.2 copy-start
  5.3 1.2 copy-start.1
  6.5 1.2 copy-start.2

commit v2 on v1

v2 whole, which is shorter than its diff:
```python
import functools

import jax
import jax.numpy as jnp
from jax import lax
from jax.experimental import pallas as pl
from jax.experimental.pallas import tpu as pltpu
from jax.sharding import PartitionSpec as P

first_decay = 0.9
second_decay = 0.95
adam_epsilon = 1e-08
ROWS = 16
COLS = 512
PARTS = 1
VMEM_BYTES = 60 * 1024 * 1024


def dot(a, b, contract_a, contract_b):
    return lax.dot_general(
        a, b, (((contract_a,), (contract_b,)), ((), ())), preferred_element_type=jnp.float32
    )


def kernel(
    places,
    n_hidden,
    capacity,
    swap_ref,
    ids_ref,
    route_ref,
    acts_ref,
    gout_ref,
    w_hbm,
    m_hbm,
    v_hbm,
    comb_ref,
    ggu_ref,
    upd_hbm,
    w_here,
    m_here,
    v_here,
    table,
    h_send,
    h_recv,
    g_send,
    g_recv,
    w_send,
    w_recv,
    h_own,
    h_all,
    y_send,
    y_recv,
    gw_send,
    gw_recv,
    gh_send,
    gh_recv,
    gr_send,
    gr_recv,
    u_here,
    u_mid,
    u_out,
    partner_row,
    partner_ref,
    local_sem,
    send_sem,
    recv_sem,
):
    me = lax.axis_index("expert")
    mine = lax.axis_index("hidden")
    tok = ids_ref.shape[1]
    count = 2 * tok
    slots = places * capacity
    unit = h_own.shape[1]
    feat = gout_ref.shape[0]
    row_groups = w_here.shape[0] // ROWS
    col_groups = w_here.shape[1] // COLS
    stride = places // row_groups

    def far_first(at, step, length):
        near = length - step
        half = (near + 1) // 2
        return lax.rem(at + half + (1 - lax.rem(near, 2)) * (length - 2 * half), length)

    def expert_peer(step):
        return far_first(me, step, places)

    def hidden_peer(step):
        return lax.rem(mine + step, n_hidden)

    barrier = pltpu.get_barrier_semaphore()

    def greet_expert(step, carry):
        pl.semaphore_signal(barrier, inc=1, device_id={"expert": expert_peer(step)})
        return carry

    def greet_hidden(step, carry):
        pl.semaphore_signal(barrier, inc=1, device_id={"hidden": hidden_peer(step)})
        return carry

    lax.fori_loop(1, places, greet_expert, 0)
    lax.fori_loop(1, n_hidden, greet_hidden, 0)

    loads = [
        pltpu.make_async_copy(src, dst, local_sem.at[at])
        for at, (src, dst) in enumerate(((w_hbm, w_here), (m_hbm, m_here), (v_hbm, v_here)))
    ]
    for load in loads:
        load.start()

    ids = jnp.concatenate([ids_ref[0:1, :], ids_ref[1:2, :]], axis=1)
    hot = (lax.broadcasted_iota(jnp.int32, (places, count), 0) == ids).astype(jnp.float32)
    earlier = (
        lax.broadcasted_iota(jnp.int32, (count, count), 0)
        < lax.broadcasted_iota(jnp.int32, (count, count), 1)
    ).astype(jnp.bfloat16)
    before = dot(hot.astype(jnp.bfloat16), earlier, 1, 0)
    rank = jnp.sum(before * hot, axis=0, keepdims=True).astype(jnp.int32)
    slot = ids * capacity + rank
    table[...] = (lax.broadcasted_iota(jnp.int32, (slots, count), 0) == slot).astype(jnp.bfloat16)

    def gate_and_up(choice):
        at = choice * 2 * unit
        gate = acts_ref[:, at : at + unit].astype(jnp.float32)
        up = acts_ref[:, at + unit : at + 2 * unit].astype(jnp.float32)
        return gate, up

    rows = []
    for choice in range(2):
        gate, up = gate_and_up(choice)
        rows.append((gate * jax.nn.sigmoid(gate) * up).astype(jnp.bfloat16))
    placed = dot(table[...], jnp.concatenate(rows, axis=0), 1, 0)
    h_send[...] = placed.reshape(places, capacity, unit).astype(jnp.bfloat16)

    unsent = []

    def arrived(dst, at):
        pltpu.make_async_copy(dst, dst, recv_sem.at[at]).wait()

    def sent(src, at):
        pltpu.make_async_copy(src, src, send_sem.at[at]).wait()

    def to_experts(src, dst, at, first=1, last=places):
        def send(step, carry):
            peer = expert_peer(step)
            pltpu.make_async_remote_copy(
                src_ref=src.at[peer],
                dst_ref=dst.at[me],
                send_sem=send_sem.at[at],
                recv_sem=recv_sem.at[at],
                device_id={"expert": peer},
            ).start()
            return carry

        lax.fori_loop(first, last, send, 0)
        if last == places:
            pltpu.make_async_copy(src.at[me], dst.at[me], recv_sem.at[at]).start()
            unsent.append((dst.at[pl.ds(0, places - 1)], at))

    def to_hidden(src, dst, at, block=True):
        def send(step, carry):
            peer = hidden_peer(step)
            pltpu.make_async_remote_copy(
                src_ref=src.at[peer] if block else src,
                dst_ref=dst.at[mine],
                send_sem=send_sem.at[at],
                recv_sem=recv_sem.at[at],
                device_id={"hidden": peer},
            ).start()
            return carry

        lax.fori_loop(1, n_hidden, send, 0)
        pltpu.make_async_copy(
            src.at[mine] if block else src, dst.at[mine], recv_sem.at[at]
        ).start()
        unsent.append((dst.at[pl.ds(0, n_hidden - 1)], at))

    rows = [
        (route_ref[choice : choice + 1, :] * gout_ref[...].astype(jnp.float32)).astype(jnp.bfloat16)
        for choice in range(2)
    ]
    placed = dot(table[...], jnp.concatenate(rows, axis=1), 1, 1)
    g_send[...] = placed.reshape(places, capacity, feat).astype(jnp.bfloat16)
    loads[0].wait()
    for block in range(n_hidden):
        w_send[block] = w_here[:, block * feat : (block + 1) * feat]

    def send_blocks(product, src, dst, at):
        def send(step, carry):
            peer = hidden_peer(step)
            src[peer] = product(peer).astype(jnp.bfloat16)
            pltpu.make_async_remote_copy(
                src_ref=src.at[peer],
                dst_ref=dst.at[mine],
                send_sem=send_sem.at[at],
                recv_sem=recv_sem.at[at],
                device_id={"hidden": peer},
            ).start()
            return carry

        lax.fori_loop(1, n_hidden, send, 0)
        src[mine] = product(mine).astype(jnp.bfloat16)
        pltpu.make_async_copy(src.at[mine], dst.at[mine], recv_sem.at[at]).start()
        unsent.append((dst.at[pl.ds(0, n_hidden - 1)], at))

    pl.semaphore_wait(barrier, places + n_hidden - 2)
    to_hidden(w_send, w_recv, 1)
    to_experts(h_send, h_recv, 0)
    to_experts(g_send, g_recv, 2)

    place = lax.broadcasted_iota(jnp.int32, (128, swap_ref.shape[1]), 0)
    left, right = swap_ref[0:1, :], swap_ref[1:2, :]
    trades = jnp.where(place == left, right, 0) + jnp.where(place == right, left, 0)
    trades = jnp.sum(trades, axis=1, keepdims=True)
    partner_row[...] = jnp.broadcast_to(trades, (128, 128)).T[0:1, :]
    table_copy = pltpu.make_async_copy(partner_row, partner_ref, local_sem.at[3])
    table_copy.start()

    arrived(h_recv, 0)
    h_own[...] = h_recv[...].astype(jnp.float32).reshape(slots, unit).astype(jnp.bfloat16)
    to_hidden(h_own, h_all, 3, block=False)
    arrived(w_recv, 1)
    arrived(h_all, 3)
    w_all = w_recv[...].reshape(n_hidden * unit, feat)
    h_cat = jnp.concatenate([h_all[block] for block in range(n_hidden)], axis=1)
    y_send[...] = dot(h_cat, w_all, 1, 0).reshape(places, capacity, feat).astype(jnp.bfloat16)
    to_experts(y_send, y_recv, 4, 1, places // 2)
    arrived(g_recv, 2)
    grads = g_recv[...].astype(jnp.float32).reshape(slots, feat).astype(jnp.bfloat16)
    send_blocks(lambda block: dot(h_all[block], grads, 0, 0), gw_send, gw_recv, 5)
    to_experts(y_send, y_recv, 4, places // 2, places)

    arrived(gw_recv, 5)
    loads[1].wait()
    loads[2].wait()
    is_mid = lax.rem(me, stride) < col_groups
    my_row = pl.multiple_of((me // stride) * ROWS, ROWS)
    my_col = lax.rem(me, stride) * COLS
    wide = COLS // PARTS

    def column_at(base, part):
        return pl.ds(pl.multiple_of(base + part * wide, wide), wide)

    def send_rows(group, part):
        at = pl.multiple_of(group * ROWS, ROWS)

        def send(col, carry):
            peer = group * stride + col
            chunk = u_here.at[pl.ds(at, ROWS), column_at(col * COLS, part)]

            @pl.when(peer == me)
            def _():
                pltpu.make_async_copy(chunk, u_mid.at[part, me], recv_sem.at[8 + part]).start()

            @pl.when(peer != me)
            def _():
                pltpu.make_async_remote_copy(
                    src_ref=chunk,
                    dst_ref=u_mid.at[part, me],
                    send_sem=send_sem.at[8 + part],
                    recv_sem=recv_sem.at[8 + part],
                    device_id={"expert": peer},
                ).start()

            return carry

        lax.fori_loop(0, col_groups, send, 0)

    def row_group(step):
        return far_first(me // stride, step, row_groups)

    def update_rows(step, carry):
        group = row_group(step)
        at = pl.multiple_of(group * ROWS, ROWS)
        for pair in range(n_hidden // 2):
            span = slice(pair * 2 * feat, (pair + 1) * 2 * feat)
            grad = jnp.concatenate(
                [
                    gw_recv[2 * pair, pl.ds(at, ROWS), :],
                    gw_recv[2 * pair + 1, pl.ds(at, ROWS), :],
                ],
                axis=1,
            ).astype(jnp.float32)
            first = m_here[pl.ds(at, ROWS), span].astype(jnp.float32)
            second = v_here[pl.ds(at, ROWS), span].astype(jnp.float32)
            first_new = first_decay * first + (1.0 - first_decay) * grad
            second_new = second_decay * second + (1.0 - second_decay) * grad * grad
            u_here[pl.ds(at, ROWS), span] = (
                first_new / (jnp.sqrt(second_new) + adam_epsilon)
            ).astype(jnp.bfloat16)
        send_rows(group, 0)
        return carry

    lax.fori_loop(1, row_groups + 1, update_rows, 0)
    send_blocks(lambda block: dot(grads, w_recv[block], 1, 1), gh_send, gh_recv, 6)

    arrived(y_recv, 4)
    back = y_recv[...].astype(jnp.float32).reshape(slots, feat).astype(jnp.bfloat16)
    picked = dot(back, table[...], 0, 0)
    comb_ref[...] = (
        route_ref[0:1, :] * picked[:, :tok] + route_ref[1:2, :] * picked[:, tok:]
    ).astype(jnp.bfloat16)
    arrived(gh_recv, 6)
    total = gh_recv[0].astype(jnp.float32)
    for block in range(1, n_hidden):
        total = total + gh_recv[block].astype(jnp.float32)
    gr_send[...] = total.reshape(places, capacity, unit).astype(jnp.bfloat16)
    to_experts(gr_send, gr_recv, 7)
    table_copy.wait()

    @pl.when(is_mid)
    def _():
        for part in range(PARTS):
            arrived(u_mid.at[part], 8 + part)
            target = upd_hbm.at[pl.ds(my_row, ROWS), column_at(my_col, part)]

            def forward(step, carry, part=part, target=target):
                peer = expert_peer(step)
                u_out[part, peer] = u_mid[part, partner_ref[0, peer]]
                pltpu.make_async_remote_copy(
                    src_ref=u_out.at[part, peer],
                    dst_ref=target,
                    send_sem=send_sem.at[8 + PARTS],
                    recv_sem=recv_sem.at[8 + PARTS],
                    device_id={"expert": peer},
                ).start()
                return carry

            lax.fori_loop(1, places, forward, 0)
            u_out[part, me] = u_mid[part, partner_ref[0, me]]
            pltpu.make_async_copy(u_out.at[part, me], target, recv_sem.at[8 + PARTS]).start()

    arrived(gr_recv, 7)
    back = gr_recv[...].astype(jnp.float32).reshape(slots, unit).astype(jnp.bfloat16)
    picked = dot(table[...], back, 0, 0)
    for choice in range(2):
        gate, up = gate_and_up(choice)
        sig = jax.nn.sigmoid(gate)
        grad_hidden = picked[choice * tok : (choice + 1) * tok]
        at = choice * 2 * unit
        ggu_ref[:, at : at + unit] = (
            grad_hidden * up * sig * (1.0 + gate * (1.0 - sig))
        ).astype(jnp.bfloat16)
        ggu_ref[:, at + unit : at + 2 * unit] = (grad_hidden * (gate * sig)).astype(jnp.bfloat16)
    for src, at in unsent:
        sent(src, at)

    arrived(upd_hbm, 8 + PARTS)

    @pl.when(is_mid)
    def _():
        for part in range(PARTS):
            sent(u_mid.at[part, pl.ds(0, row_groups * col_groups - 1)], 8 + part)
            sent(u_out.at[part, pl.ds(0, places - 1)], 8 + PARTS)

    @pl.when(jnp.logical_not(is_mid))
    def _():
        for part in range(PARTS):
            sent(u_mid.at[part, pl.ds(0, row_groups * col_groups)], 8 + part)


def local(
    swap_pairs,
    expert_ids,
    route_weights,
    gate_up,
    grad_out,
    down_weight,
    first_moment,
    second_moment,
):
    places = lax.axis_size("expert")
    n_hidden = lax.axis_size("hidden")
    tok, top = expert_ids.shape
    unit, depth = down_weight.shape[1:]
    feat = grad_out.shape[1]
    capacity = 2 * tok * top // places
    slots = places * capacity
    bf16 = jnp.bfloat16
    vmem = pl.BlockSpec(memory_space=pltpu.VMEM)
    anywhere = pl.BlockSpec(memory_space=pl.ANY)
    scratch = [
        ((unit, depth), bf16),
        ((unit, depth), bf16),
        ((unit, depth), bf16),
        ((slots, tok * top), bf16),
        ((places, capacity, unit), bf16),
        ((places, capacity, unit), bf16),
        ((places, capacity, feat), bf16),
        ((places, capacity, feat), bf16),
        ((n_hidden, unit, feat), bf16),
        ((n_hidden, unit, feat), bf16),
        ((slots, unit), bf16),
        ((n_hidden, slots, unit), bf16),
        ((places, capacity, feat), bf16),
        ((places, capacity, feat), bf16),
        ((n_hidden, unit, feat), bf16),
        ((n_hidden, unit, feat), bf16),
        ((n_hidden, slots, unit), bf16),
        ((n_hidden, slots, unit), bf16),
        ((places, capacity, unit), bf16),
        ((places, capacity, unit), bf16),
        ((unit, depth), bf16),
        ((PARTS, places, ROWS, COLS // PARTS), bf16),
        ((PARTS, places, ROWS, COLS // PARTS), bf16),
        ((1, 128), jnp.int32),
    ]
    combined, grads, update = pl.pallas_call(
        functools.partial(kernel, places, n_hidden, capacity),
        out_shape=(
            jax.ShapeDtypeStruct((feat, tok), bf16),
            jax.ShapeDtypeStruct((tok, top * 2 * unit), bf16),
            jax.ShapeDtypeStruct((unit, depth), bf16),
        ),
        in_specs=[vmem] * 5 + [anywhere] * 3,
        out_specs=(vmem, vmem, anywhere),
        scratch_shapes=[pltpu.VMEM(shape, kind) for shape, kind in scratch]
        + [
            pltpu.SMEM((1, 128), jnp.int32),
            pltpu.SemaphoreType.DMA((4,)),
            pltpu.SemaphoreType.DMA((9 + PARTS,)),
            pltpu.SemaphoreType.DMA((9 + PARTS,)),
        ],
        compiler_params=pltpu.CompilerParams(
            collective_id=0, has_side_effects=True, vmem_limit_bytes=VMEM_BYTES
        ),
    )(
        swap_pairs.T,
        expert_ids.T,
        route_weights.T,
        gate_up.reshape(tok, top * 2 * unit),
        grad_out.T,
        down_weight[0],
        first_moment[0],
        second_moment[0],
    )
    return combined.T, grads.reshape(tok, top, 2, unit), update[None]


def solution(mesh):
    placed = (
        P(),
        P("expert", None),
        P("expert", None),
        P("expert", None, None, "hidden"),
        P("expert", "hidden"),
        P("expert", "hidden", None),
        P("expert", "hidden", None),
        P("expert", "hidden", None),
    )
    return jax.shard_map(
        local,
        mesh=mesh,
        in_specs=placed,
        out_specs=(
            P("expert", "hidden"),
            P("expert", None, None, "hidden"),
            P("expert", "hidden", None),
        ),
        check_vma=False,
    )
```

time: 183 us -> 176 us (0.962)
  Pallas kernels: 172 us -> 168 us
  local copies, waits for them, and re-layouts: 9.24 us -> 6.05 us
    unnamed x15 -> x4, local copies, waits for them, and re-layouts: 7.74 us -> 2.81 us
    pallas_call x1, Pallas kernels: 172 us -> 168 us  [local(): pl.pallas_call(functools.partial(kernel, places, n_hidden, capacity), out...]
where the time goes in v2:
time: 176 us; the launch traced here: 175 us
  Pallas kernels  168 us (95%)
  local copies, waits for them, and re-layouts  6.05 us (3%)
    pallas_call x1, Pallas kernels, local(): pl.pallas_call(functools.partial(kernel, places, n_hidden, capacity), out...  168 us

profile of v2, /device:TPU:24, one launch (start us, length us, event | category | flops | bytes accessed | tf_op | source)
XLA Modules:
  0.0 175.1 jit_solution(12921320734004708350)
XLA Ops:
  0.6 1.6 reshape.12.acts_ref
  2.2 168.4 %shard_map.103 = (bf16[448,128]{1,0:T(8,128)(2,1)}, bf16[128,512]{1,0:T(8,128)(2,1)}, bf16[128,3584]{1,0:T(8,128)(2,1)}) custom-call(s32[2,32]{1,0:T(2,128)} %bitcast.15, s32[2,128]{1,0:T(2,128)} %bitcast.16, f32[2,128]{1,0:T(2,128)} %bitcast.17, bf16[128,512]{1,0:T(8,128)(2,1)} %reshape.12.acts_ref, bf16[448,128]{1,0:T(8,128)(2,1)} %bitcast.14, ...), custom_call_target="tpu_custom_call" | custom-call | tf_op jit(solution)/shard_map/pallas_call | solution.py:408
  170.6 0.0 copy-start
  170.7 1.6 reshape.13
  172.3 0.0 copy-done
  172.3 0.6 copy.13
  172.9 2.2 %copy.14 = bf16[1,128,3584]{2,1,0:T(8,128)(2,1)} copy(bf16[1,128,3584]{2,1,0:T(8,128)(2,1)} %bitcast.9) | data formatting | bytes 1835008
Async XLA Ops:
  170.6 1.6 copy-start

commit v3 on v2

--- a/solution.py
+++ b/solution.py
@@ -13,7 +13,8 @@
 ROWS = 16
 COLS = 512
 PARTS = 1
-VMEM_BYTES = 60 * 1024 * 1024
+LANES = 128
+VMEM_BYTES = 52 * 1024 * 1024
 
 
 def dot(a, b, contract_a, contract_b):
@@ -37,7 +38,7 @@
     comb_ref,
     ggu_ref,
     upd_hbm,
-    w_here,
+    w_all,
     m_here,
     v_here,
     table,
@@ -45,7 +46,6 @@
     h_recv,
     g_send,
     g_recv,
-    w_send,
     w_recv,
     h_own,
     h_all,
@@ -73,8 +73,8 @@
     slots = places * capacity
     unit = h_own.shape[1]
     feat = gout_ref.shape[0]
-    row_groups = w_here.shape[0] // ROWS
-    col_groups = w_here.shape[1] // COLS
+    row_groups = m_here.shape[0] // ROWS
+    col_groups = m_here.shape[1] // COLS
     stride = places // row_groups
 
     def far_first(at, step, length):
@@ -103,7 +103,7 @@
 
     loads = [
         pltpu.make_async_copy(src, dst, local_sem.at[at])
-        for at, (src, dst) in enumerate(((w_hbm, w_here), (m_hbm, m_here), (v_hbm, v_here)))
+        for at, (src, dst) in enumerate(((m_hbm, m_here), (v_hbm, v_here)))
     ]
     for load in loads:
         load.start()
@@ -157,11 +157,11 @@
             pltpu.make_async_copy(src.at[me], dst.at[me], recv_sem.at[at]).start()
             unsent.append((dst.at[pl.ds(0, places - 1)], at))
 
-    def to_hidden(src, dst, at, block=True):
+    def to_hidden(pick, dst, at):
         def send(step, carry):
             peer = hidden_peer(step)
             pltpu.make_async_remote_copy(
-                src_ref=src.at[peer] if block else src,
+                src_ref=pick(peer),
                 dst_ref=dst.at[mine],
                 send_sem=send_sem.at[at],
                 recv_sem=recv_sem.at[at],
@@ -170,9 +170,7 @@
             return carry
 
         lax.fori_loop(1, n_hidden, send, 0)
-        pltpu.make_async_copy(
-            src.at[mine] if block else src, dst.at[mine], recv_sem.at[at]
-        ).start()
+        pltpu.make_async_copy(pick(mine), dst.at[mine], recv_sem.at[at]).start()
         unsent.append((dst.at[pl.ds(0, n_hidden - 1)], at))
 
     rows = [
@@ -181,10 +179,6 @@
     ]
     placed = dot(table[...], jnp.concatenate(rows, axis=1), 1, 1)
     g_send[...] = placed.reshape(places, capacity, feat).astype(jnp.bfloat16)
-    loads[0].wait()
-    for block in range(n_hidden):
-        w_send[block] = w_here[:, block * feat : (block + 1) * feat]
-
     def send_blocks(product, src, dst, at):
         def send(step, carry):
             peer = hidden_peer(step)
@@ -204,7 +198,13 @@
         unsent.append((dst.at[pl.ds(0, n_hidden - 1)], at))
 
     pl.semaphore_wait(barrier, places + n_hidden - 2)
-    to_hidden(w_send, w_recv, 1)
+    span = w_recv.shape[2]
+
+    def weight_window(peer):
+        at = pl.multiple_of(peer * feat // LANES * LANES, LANES)
+        return w_hbm.at[:, pl.ds(at, span)]
+
+    to_hidden(weight_window, w_recv, 1)
     to_experts(h_send, h_recv, 0)
     to_experts(g_send, g_recv, 2)
 
@@ -218,12 +218,21 @@
 
     arrived(h_recv, 0)
     h_own[...] = h_recv[...].astype(jnp.float32).reshape(slots, unit).astype(jnp.bfloat16)
-    to_hidden(h_own, h_all, 3, block=False)
+    to_hidden(lambda peer: h_own, h_all, 3)
     arrived(w_recv, 1)
+    shift = span - feat
+
+    @pl.when(lax.rem(mine * feat, LANES) == 0)
+    def _():
+        w_all[...] = w_recv[:, :, :feat]
+
+    @pl.when(lax.rem(mine * feat, LANES) != 0)
+    def _():
+        w_all[...] = w_recv[:, :, shift:]
+
     arrived(h_all, 3)
-    w_all = w_recv[...].reshape(n_hidden * unit, feat)
     h_cat = jnp.concatenate([h_all[block] for block in range(n_hidden)], axis=1)
-    y_send[...] = dot(h_cat, w_all, 1, 0).reshape(places, capacity, feat).astype(jnp.bfloat16)
+    y_send[...] = dot(h_cat, w_all[...].reshape(n_hidden * unit, feat), 1, 0).reshape(places, capacity, feat).astype(jnp.bfloat16)
     to_experts(y_send, y_recv, 4, 1, places // 2)
     arrived(g_recv, 2)
     grads = g_recv[...].astype(jnp.float32).reshape(slots, feat).astype(jnp.bfloat16)
@@ -231,8 +240,8 @@
     to_experts(y_send, y_recv, 4, places // 2, places)
 
     arrived(gw_recv, 5)
-    loads[1].wait()
-    loads[2].wait()
+    for load in loads:
+        load.wait()
     is_mid = lax.rem(me, stride) < col_groups
     my_row = pl.multiple_of((me // stride) * ROWS, ROWS)
     my_col = lax.rem(me, stride) * COLS
@@ -292,7 +301,7 @@
         return carry
 
     lax.fori_loop(1, row_groups + 1, update_rows, 0)
-    send_blocks(lambda block: dot(grads, w_recv[block], 1, 1), gh_send, gh_recv, 6)
+    send_blocks(lambda block: dot(grads, w_all[block], 1, 1), gh_send, gh_recv, 6)
 
     arrived(y_recv, 4)
     back = y_recv[...].astype(jnp.float32).reshape(slots, feat).astype(jnp.bfloat16)
@@ -305,6 +314,17 @@
     for block in range(1, n_hidden):
         total = total + gh_recv[block].astype(jnp.float32)
     gr_send[...] = total.reshape(places, capacity, unit).astype(jnp.bfloat16)
+
+    @pl.when(is_mid)
+    def _():
+        for part in range(PARTS):
+            sent(u_mid.at[part, pl.ds(0, row_groups * col_groups - 1)], 8 + part)
+
+    @pl.when(jnp.logical_not(is_mid))
+    def _():
+        for part in range(PARTS):
+            sent(u_mid.at[part, pl.ds(0, row_groups * col_groups)], 8 + part)
+
     to_experts(gr_send, gr_recv, 7)
     table_copy.wait()
 
@@ -350,13 +370,7 @@
     @pl.when(is_mid)
     def _():
         for part in range(PARTS):
-            sent(u_mid.at[part, pl.ds(0, row_groups * col_groups - 1)], 8 + part)
             sent(u_out.at[part, pl.ds(0, places - 1)], 8 + PARTS)
-
-    @pl.when(jnp.logical_not(is_mid))
-    def _():
-        for part in range(PARTS):
-            sent(u_mid.at[part, pl.ds(0, row_groups * col_groups)], 8 + part)
 
 
 def local(
@@ -380,7 +394,7 @@
     vmem = pl.BlockSpec(memory_space=pltpu.VMEM)
     anywhere = pl.BlockSpec(memory_space=pl.ANY)
     scratch = [
-        ((unit, depth), bf16),
+        ((n_hidden, unit, feat), bf16),
         ((unit, depth), bf16),
         ((unit, depth), bf16),
         ((slots, tok * top), bf16),
@@ -388,8 +402,7 @@
         ((places, capacity, unit), bf16),
         ((places, capacity, feat), bf16),
         ((places, capacity, feat), bf16),
-        ((n_hidden, unit, feat), bf16),
-        ((n_hidden, unit, feat), bf16),
+        ((n_hidden, unit, -(-feat // LANES) * LANES), bf16),
         ((slots, unit), bf16),
         ((n_hidden, slots, unit), bf16),
         ((places, capacity, feat), bf16),

time: 176 us -> 173 us (0.983)
  local copies, waits for them, and re-layouts: 6.05 us -> 3.3 us
where the time goes in v3:
time: 173 us
  Pallas kernels  169 us (98%)
  local copies, waits for them, and re-layouts  3.3 us (2%)
    pallas_call x1, Pallas kernels, local(): pl.pallas_call(functools.partial(kernel, places, n_hidden, capacity), out...  169 us

profile of v3, /device:TPU:24, one launch (start us, length us, event | category | flops | bytes accessed | tf_op | source)
XLA Modules:
  0.0 172.7 jit_solution(6409357560934601248)
XLA Ops:
  0.6 0.0 copy-start
  0.6 0.0 copy-start.1
  0.7 0.0 copy-start.2
  0.7 0.0 copy-start.3
  0.7 1.0 reshape.12.acts_ref
  1.7 0.0 copy-done
  1.7 0.0 copy-done.1
  1.7 0.0 copy-done.2
  1.7 0.0 copy-done.3
  1.7 168.7 %shard_map.103 = (bf16[448,128]{1,0:T(8,128)(2,1)S(1)}, bf16[128,512]{1,0:T(8,128)(2,1)S(1)}, bf16[128,3584]{1,0:T(8,128)(2,1)S(1)}) custom-call(s32[2,32]{1,0:T(2,128)S(1)} %bitcast.12, s32[2,128]{1,0:T(2,128)S(1)} %bitcast.13, f32[2,128]{1,0:T(2,128)S(1)} %bitcast.14, bf16[128,512]{1,0:T(8,128)(2,1)S(1)} %reshape.12.acts_ref, ...), custom_call_target="tpu_custom_call" | custom-call | tf_op jit(solution)/shard_map/pallas_call | solution.py:421
  170.4 0.7 reshape.13
  171.1 0.6 copy.13
  171.8 0.9 copy.14
Async XLA Ops:
  0.6 1.1 copy-start
  0.6 1.1 copy-start.1
  0.7 1.1 copy-start.2
  0.7 1.1 copy-start.3

commit v4 on v3

--- a/solution.py
+++ b/solution.py
@@ -242,9 +242,17 @@
     arrived(gw_recv, 5)
     for load in loads:
         load.wait()
-    is_mid = lax.rem(me, stride) < col_groups
-    my_row = pl.multiple_of((me // stride) * ROWS, ROWS)
-    my_col = lax.rem(me, stride) * COLS
+
+    def spare_seat(group):
+        return stride - 1 - 2 * lax.rem(group, stride // 2)
+
+    def past_spare(at, group):
+        return (at + stride - spare_seat(group)) // stride
+
+    my_group, my_seat = me // stride, lax.rem(me, stride)
+    is_mid = my_seat != spare_seat(my_group)
+    my_row = pl.multiple_of(my_group * ROWS, ROWS)
+    my_col = (my_seat - past_spare(my_seat, my_group)) * COLS
     wide = COLS // PARTS
 
     def column_at(base, part):
@@ -254,7 +262,7 @@
         at = pl.multiple_of(group * ROWS, ROWS)
 
         def send(col, carry):
-            peer = group * stride + col
+            peer = group * stride + col + past_spare(col, group)
             chunk = u_here.at[pl.ds(at, ROWS), column_at(col * COLS, part)]
 
             @pl.when(peer == me)

time: 173 us -> 169 us (0.977)
  Pallas kernels: 169 us -> 164 us
    pallas_call x1, Pallas kernels: 169 us -> 164 us  [local(): pl.pallas_call(functools.partial(kernel, places, n_hidden, capacity), out...]
where the time goes in v4:
time: 169 us; the launch traced here: 168 us
  Pallas kernels  164 us (97%)
  local copies, waits for them, and re-layouts  3.3 us (2%)
    pallas_call x1, Pallas kernels, local(): pl.pallas_call(functools.partial(kernel, places, n_hidden, capacity), out...  164 us

profile of v4, /device:TPU:24, one launch (start us, length us, event | category | flops | bytes accessed | tf_op | source)
XLA Modules:
  0.0 168.3 jit_solution(213247846320221777)
XLA Ops:
  0.6 0.0 copy-start
  0.6 0.0 copy-start.1
  0.7 0.0 copy-start.2
  0.7 0.0 copy-start.3
  0.7 1.0 reshape.12.acts_ref
  1.7 0.0 copy-done
  1.7 0.0 copy-done.1
  1.7 0.0 copy-done.2
  1.7 0.0 copy-done.3
  1.7 164.3 %shard_map.103 = (bf16[448,128]{1,0:T(8,128)(2,1)S(1)}, bf16[128,512]{1,0:T(8,128)(2,1)S(1)}, bf16[128,3584]{1,0:T(8,128)(2,1)S(1)}) custom-call(s32[2,32]{1,0:T(2,128)S(1)} %bitcast.12, s32[2,128]{1,0:T(2,128)S(1)} %bitcast.13, f32[2,128]{1,0:T(2,128)S(1)} %bitcast.14, bf16[128,512]{1,0:T(8,128)(2,1)S(1)} %reshape.12.acts_ref, ...), custom_call_target="tpu_custom_call" | custom-call | tf_op jit(solution)/shard_map/pallas_call | solution.py:429
  166.1 0.7 reshape.13
  166.8 0.6 copy.13
  167.4 0.9 copy.14
Async XLA Ops:
  0.6 1.1 copy-start
  0.6 1.1 copy-start.1
  0.7 1.1 copy-start.2
  0.7 1.1 copy-start.3

commit v5 on v4

--- a/solution.py
+++ b/solution.py
@@ -14,6 +14,8 @@
 COLS = 512
 PARTS = 1
 LANES = 128
+GRADS = 12
+OUTPUTS = 16
 VMEM_BYTES = 52 * 1024 * 1024
 
 
@@ -46,11 +48,13 @@
     h_recv,
     g_send,
     g_recv,
+    g_rows,
     w_recv,
     h_own,
     h_all,
     y_send,
     y_recv,
+    y_rows,
     gw_send,
     gw_recv,
     gh_send,
@@ -140,7 +144,7 @@
     def sent(src, at):
         pltpu.make_async_copy(src, src, send_sem.at[at]).wait()
 
-    def to_experts(src, dst, at, first=1, last=places):
+    def to_experts(src, dst, at):
         def send(step, carry):
             peer = expert_peer(step)
             pltpu.make_async_remote_copy(
@@ -152,10 +156,9 @@
             ).start()
             return carry
 
-        lax.fori_loop(first, last, send, 0)
-        if last == places:
-            pltpu.make_async_copy(src.at[me], dst.at[me], recv_sem.at[at]).start()
-            unsent.append((dst.at[pl.ds(0, places - 1)], at))
+        lax.fori_loop(1, places, send, 0)
+        pltpu.make_async_copy(src.at[me], dst.at[me], recv_sem.at[at]).start()
+        unsent.append((dst.at[pl.ds(0, places - 1)], at))
 
     def to_hidden(pick, dst, at):
         def send(step, carry):
@@ -178,7 +181,91 @@
         for choice in range(2)
     ]
     placed = dot(table[...], jnp.concatenate(rows, axis=1), 1, 1)
-    g_send[...] = placed.reshape(places, capacity, feat).astype(jnp.bfloat16)
+    core = lax.rem(me, 2)
+    span = g_recv.shape[2]
+    rest = 2 * feat - span
+
+    def paired(rows):
+        rows = rows.reshape(places // 2, 2, capacity, feat)
+        return jnp.concatenate([rows[:, 0], rows[:, 1]], axis=2).astype(jnp.bfloat16)
+
+    def to_chips(src, dst, at, first=1, last=places // 2):
+        def to_core(chip, side):
+            if side == 0:
+                part, target = src.at[chip, :, pl.ds(0, span)], dst.at[me]
+            else:
+                part, target = src.at[chip, :, pl.ds(span, rest)], dst.at[me, :, pl.ds(span - rest, rest)]
+            return part, target
+
+        def start(chip, side):
+            part, target = to_core(chip, side)
+            pltpu.make_async_remote_copy(
+                src_ref=part,
+                dst_ref=target,
+                send_sem=send_sem.at[at + side],
+                recv_sem=recv_sem.at[at],
+                device_id={"expert": 2 * chip + side},
+            ).start()
+
+        def send(step, carry):
+            chip = far_first(me // 2, step, places // 2)
+            start(chip, 0)
+            start(chip, 1)
+            return carry
+
+        lax.fori_loop(first, last, send, 0)
+        if last == places // 2:
+            for side in range(2):
+
+                @pl.when(core == side)
+                def _(side=side):
+                    start(me // 2, 1 - side)
+                    part, target = to_core(me // 2, side)
+                    pltpu.make_async_copy(part, target, recv_sem.at[at]).start()
+
+    def from_chips(dst, rows, at):
+        def unpack(offset):
+            return dst[:, :, offset : offset + feat].astype(jnp.float32).reshape(slots, feat).astype(jnp.bfloat16)
+
+        seam = dst.at[:, :, pl.ds(span - LANES, LANES)]
+        other = dst.at[:, :, pl.ds(0, LANES)]
+
+        @pl.when(core == 0)
+        def _():
+            arrived(dst, at)
+            if rest < span:
+                pltpu.make_async_remote_copy(
+                    src_ref=seam,
+                    dst_ref=other,
+                    send_sem=send_sem.at[at + 2],
+                    recv_sem=recv_sem.at[at + 1],
+                    device_id={"expert": me + 1},
+                ).start()
+            rows[...] = unpack(0)
+
+        @pl.when(core == 1)
+        def _():
+            arrived(dst.at[:, :, pl.ds(span - rest, rest)], at)
+            if rest < span:
+                arrived(other, at + 1)
+            rows[...] = unpack(span - feat)
+
+    def chips_sent(dst, at):
+        half = places // 2
+        for side in range(2):
+
+            @pl.when(core == side)
+            def _(side=side):
+                sent(dst.at[pl.ds(0, half - (side == 0))], at)
+                sent(dst.at[pl.ds(0, half - (side == 1)), :, pl.ds(0, rest)], at + 1)
+
+        if rest < span:
+
+            @pl.when(core == 0)
+            def _():
+                sent(dst.at[:, :, pl.ds(0, LANES)], at + 2)
+
+    g_send[...] = paired(placed)
     def send_blocks(product, src, dst, at):
         def send(step, carry):
             peer = hidden_peer(step)
@@ -198,15 +285,13 @@
         unsent.append((dst.at[pl.ds(0, n_hidden - 1)], at))
 
     pl.semaphore_wait(barrier, places + n_hidden - 2)
-    span = w_recv.shape[2]
-
     def weight_window(peer):
         at = pl.multiple_of(peer * feat // LANES * LANES, LANES)
         return w_hbm.at[:, pl.ds(at, span)]
 
     to_hidden(weight_window, w_recv, 1)
     to_experts(h_send, h_recv, 0)
-    to_experts(g_send, g_recv, 2)
+    to_chips(g_send, g_recv, GRADS)
 
     place = lax.broadcasted_iota(jnp.int32, (128, swap_ref.shape[1]), 0)
     left, right = swap_ref[0:1, :], swap_ref[1:2, :]
@@ -232,12 +317,12 @@
 
     arrived(h_all, 3)
     h_cat = jnp.concatenate([h_all[block] for block in range(n_hidden)], axis=1)
-    y_send[...] = dot(h_cat, w_all[...].reshape(n_hidden * unit, feat), 1, 0).reshape(places, capacity, feat).astype(jnp.bfloat16)
-    to_experts(y_send, y_recv, 4, 1, places // 2)
-    arrived(g_recv, 2)
-    grads = g_recv[...].astype(jnp.float32).reshape(slots, feat).astype(jnp.bfloat16)
+    y_send[...] = paired(dot(h_cat, w_all[...].reshape(n_hidden * unit, feat), 1, 0))
+    to_chips(y_send, y_recv, OUTPUTS, 1, places // 4)
+    from_chips(g_recv, g_rows, GRADS)
+    grads = g_rows[...]
     send_blocks(lambda block: dot(h_all[block], grads, 0, 0), gw_send, gw_recv, 5)
-    to_experts(y_send, y_recv, 4, places // 2, places)
+    to_chips(y_send, y_recv, OUTPUTS, places // 4, places // 2)
 
     arrived(gw_recv, 5)
     for load in loads:
@@ -311,8 +396,8 @@
     lax.fori_loop(1, row_groups + 1, update_rows, 0)
     send_blocks(lambda block: dot(grads, w_all[block], 1, 1), gh_send, gh_recv, 6)
 
-    arrived(y_recv, 4)
-    back = y_recv[...].astype(jnp.float32).reshape(slots, feat).astype(jnp.bfloat16)
+    from_chips(y_recv, y_rows, OUTPUTS)
+    back = y_rows[...]
     picked = dot(back, table[...], 0, 0)
     comb_ref[...] = (
         route_ref[0:1, :] * picked[:, :tok] + route_ref[1:2, :] * picked[:, tok:]
@@ -372,6 +457,8 @@
         ggu_ref[:, at + unit : at + 2 * unit] = (grad_hidden * (gate * sig)).astype(jnp.bfloat16)
     for src, at in unsent:
         sent(src, at)
+    chips_sent(g_recv, GRADS)
+    chips_sent(y_recv, OUTPUTS)
 
     arrived(upd_hbm, 8 + PARTS)
 
@@ -408,13 +495,15 @@
         ((slots, tok * top), bf16),
         ((places, capacity, unit), bf16),
         ((places, capacity, unit), bf16),
-        ((places, capacity, feat), bf16),
-        ((places, capacity, feat), bf16),
+        ((places // 2, capacity, 2 * feat), bf16),
+        ((places, capacity, -(-feat // LANES) * LANES), bf16),
+        ((slots, feat), bf16),
         ((n_hidden, unit, -(-feat // LANES) * LANES), bf16),
         ((slots, unit), bf16),
         ((n_hidden, slots, unit), bf16),
-        ((places, capacity, feat), bf16),
-        ((places, capacity, feat), bf16),
+        ((places // 2, capacity, 2 * feat), bf16),
+        ((places, capacity, -(-feat // LANES) * LANES), bf16),
+        ((slots, feat), bf16),
         ((n_hidden, unit, feat), bf16),
         ((n_hidden, unit, feat), bf16),
         ((n_hidden, slots, unit), bf16),
@@ -439,8 +528,8 @@
         + [
             pltpu.SMEM((1, 128), jnp.int32),
             pltpu.SemaphoreType.DMA((4,)),
-            pltpu.SemaphoreType.DMA((9 + PARTS,)),
-            pltpu.SemaphoreType.DMA((9 + PARTS,)),
+            pltpu.SemaphoreType.DMA((20,)),
+            pltpu.SemaphoreType.DMA((20,)),
         ],
         compiler_params=pltpu.CompilerParams(
             collective_id=0, has_side_effects=True, vmem_limit_bytes=VMEM_BYTES

time: 169 us -> 166 us (0.982)
  Pallas kernels: 164 us -> 161 us
    pallas_call x1, Pallas kernels: 164 us -> 161 us  [local(): pl.pallas_call(functools.partial(kernel, places, n_hidden, capacity), out...]
where the time goes in v5:
time: 166 us; the launch traced here: 165 us
  Pallas kernels  161 us (97%)
  local copies, waits for them, and re-layouts  3.3 us (2%)
    pallas_call x1, Pallas kernels, local(): pl.pallas_call(functools.partial(kernel, places, n_hidden, capacity), out...  161 us

profile of v5, /device:TPU:24, one launch (start us, length us, event | category | flops | bytes accessed | tf_op | source)
XLA Modules:
  0.0 165.3 jit_solution(7634150417196812211)
XLA Ops:
  0.6 0.0 copy-start
  0.6 0.0 copy-start.1
  0.7 0.0 copy-start.2
  0.7 0.0 copy-start.3
  0.7 1.0 reshape.12.acts_ref
  1.7 0.0 copy-done
  1.7 0.0 copy-done.1
  1.7 0.0 copy-done.2
  1.7 0.0 copy-done.3
  1.7 161.3 %shard_map.103 = (bf16[448,128]{1,0:T(8,128)(2,1)S(1)}, bf16[128,512]{1,0:T(8,128)(2,1)S(1)}, bf16[128,3584]{1,0:T(8,128)(2,1)S(1)}) custom-call(s32[2,32]{1,0:T(2,128)S(1)} %bitcast.12, s32[2,128]{1,0:T(2,128)S(1)} %bitcast.13, f32[2,128]{1,0:T(2,128)S(1)} %bitcast.14, bf16[128,512]{1,0:T(8,128)(2,1)S(1)} %reshape.12.acts_ref, ...), custom_call_target="tpu_custom_call" | custom-call | tf_op jit(solution)/shard_map/pallas_call | solution.py:518
  163.0 0.7 reshape.13
  163.7 0.6 copy.13
  164.4 0.9 copy.14
Async XLA Ops:
  0.6 1.1 copy-start
  0.6 1.1 copy-start.1
  0.7 1.1 copy-start.2
  0.7 1.1 copy-start.3

commit v6 on v5

--- a/solution.py
+++ b/solution.py
@@ -123,17 +123,17 @@
     slot = ids * capacity + rank
     table[...] = (lax.broadcasted_iota(jnp.int32, (slots, count), 0) == slot).astype(jnp.bfloat16)
 
-    def gate_and_up(choice):
-        at = choice * 2 * unit
-        gate = acts_ref[:, at : at + unit].astype(jnp.float32)
-        up = acts_ref[:, at + unit : at + 2 * unit].astype(jnp.float32)
-        return gate, up
-
-    rows = []
-    for choice in range(2):
-        gate, up = gate_and_up(choice)
-        rows.append((gate * jax.nn.sigmoid(gate) * up).astype(jnp.bfloat16))
-    placed = dot(table[...], jnp.concatenate(rows, axis=0), 1, 0)
+    def picks(kind):
+        row = lax.broadcasted_iota(jnp.int32, (count, 2 * count), 0)
+        wanted = 4 * lax.rem(row, tok) + 2 * (row // tok) + kind
+        return (lax.broadcasted_iota(jnp.int32, (count, 2 * count), 1) == wanted).astype(jnp.bfloat16)
+
+    def gate_and_up():
+        return dot(picks(0), acts_ref[...], 1, 0), dot(picks(1), acts_ref[...], 1, 0)
+
+    gate, up = gate_and_up()
+    hidden = (gate * jax.nn.sigmoid(gate) * up).astype(jnp.bfloat16)
+    placed = dot(table[...], hidden, 1, 0)
     h_send[...] = placed.reshape(places, capacity, unit).astype(jnp.bfloat16)
 
     unsent = []
@@ -318,11 +318,12 @@
     arrived(h_all, 3)
     h_cat = jnp.concatenate([h_all[block] for block in range(n_hidden)], axis=1)
     y_send[...] = paired(dot(h_cat, w_all[...].reshape(n_hidden * unit, feat), 1, 0))
-    to_chips(y_send, y_recv, OUTPUTS, 1, places // 4)
+    early = max(1, places // 8)
+    to_chips(y_send, y_recv, OUTPUTS, 1, early)
     from_chips(g_recv, g_rows, GRADS)
     grads = g_rows[...]
     send_blocks(lambda block: dot(h_all[block], grads, 0, 0), gw_send, gw_recv, 5)
-    to_chips(y_send, y_recv, OUTPUTS, places // 4, places // 2)
+    to_chips(y_send, y_recv, OUTPUTS, early, places // 2)
 
     arrived(gw_recv, 5)
     for load in loads:
@@ -445,16 +446,14 @@
 
     arrived(gr_recv, 7)
     back = gr_recv[...].astype(jnp.float32).reshape(slots, unit).astype(jnp.bfloat16)
-    picked = dot(table[...], back, 0, 0)
-    for choice in range(2):
-        gate, up = gate_and_up(choice)
-        sig = jax.nn.sigmoid(gate)
-        grad_hidden = picked[choice * tok : (choice + 1) * tok]
-        at = choice * 2 * unit
-        ggu_ref[:, at : at + unit] = (
-            grad_hidden * up * sig * (1.0 + gate * (1.0 - sig))
-        ).astype(jnp.bfloat16)
-        ggu_ref[:, at + unit : at + 2 * unit] = (grad_hidden * (gate * sig)).astype(jnp.bfloat16)
+    grad_hidden = dot(table[...], back, 0, 0)
+    gate, up = gate_and_up()
+    sig = jax.nn.sigmoid(gate)
+    grad_gate = (grad_hidden * up * sig * (1.0 + gate * (1.0 - sig))).astype(jnp.bfloat16)
+    grad_up = (grad_hidden * (gate * sig)).astype(jnp.bfloat16)
+    ggu_ref[...] = (dot(picks(0), grad_gate, 0, 0) + dot(picks(1), grad_up, 0, 0)).astype(
+        jnp.bfloat16
+    )
     for src, at in unsent:
         sent(src, at)
     chips_sent(g_recv, GRADS)
@@ -519,7 +518,7 @@
         functools.partial(kernel, places, n_hidden, capacity),
         out_shape=(
             jax.ShapeDtypeStruct((feat, tok), bf16),
-            jax.ShapeDtypeStruct((tok, top * 2 * unit), bf16),
+            jax.ShapeDtypeStruct((tok * top * 2, unit), bf16),
             jax.ShapeDtypeStruct((unit, depth), bf16),
         ),
         in_specs=[vmem] * 5 + [anywhere] * 3,
@@ -538,7 +537,7 @@
         swap_pairs.T,
         expert_ids.T,
         route_weights.T,
-        gate_up.reshape(tok, top * 2 * unit),
+        gate_up.reshape(tok * top * 2, unit),
         grad_out.T,
         down_weight[0],
         first_moment[0],

time: 166 us -> 167 us (level)
    unnamed x10 -> x13, local copies, waits for them, and re-layouts: 1.58 us -> 4.71 us
    reshape x2 -> x0, local copies, waits for them, and re-layouts: 1.71 us -> none  [the longest x1 1.02 us: local(): gate_up.reshape(tok, top * 2 * unit)]
where the time goes in v6:
time: 167 us
  Pallas kernels  161 us (96%)
  local copies, waits for them, and re-layouts  4.71 us (3%)
    pallas_call x1, Pallas kernels, local(): pl.pallas_call(functools.partial(kernel, places, n_hidden, capacity), out...  161 us
    unnamed x13, local copies, waits for them, and re-layouts  4.71 us

profile of v6, /device:TPU:24, one launch (start us, length us, event | category | flops | bytes accessed | tf_op | source)
XLA Modules:
  0.0 166.5 jit_solution(13514097887699452084)
XLA Ops:
  0.6 0.0 copy-start.3
  0.6 0.0 copy-start.4
  0.7 0.0 copy-start.2
  0.7 0.7 copy-done.3
  1.3 0.0 copy-done.4
  1.3 0.0 copy-done.2
  1.3 0.0 copy-start
  1.3 0.9 copy-done
  2.2 0.0 copy-start.1
  2.3 0.9 copy-done.1
  3.1 161.1 %shard_map.103 = (bf16[448,128]{1,0:T(8,128)(2,1)S(1)}, bf16[512,128]{1,0:T(8,128)(2,1)S(1)}, bf16[128,3584]{1,0:T(8,128)(2,1)S(1)}) custom-call(s32[2,32]{1,0:T(2,128)S(1)} %bitcast.16, s32[2,128]{1,0:T(2,128)S(1)} %bitcast.17, f32[2,128]{1,0:T(2,128)S(1)} %bitcast.18, bf16[512,128]{1,0:T(8,128)(2,1)S(1)} %bitcast.12, bf16[448,128]{1,0:T(8,128)(2,1)S(1)} %bitcast.15, ...), custom_call_target="tpu_custom_call" | custom-call | tf_op jit(solution)/shard_map/pallas_call | solution.py:517
  164.3 0.6 copy.14
  165.0 0.7 copy.15
  165.6 0.9 copy.16
Async XLA Ops:
  0.6 0.7 copy-start.3
  0.6 0.7 copy-start.4
  0.7 0.7 copy-start.2
  1.3 0.9 copy-start
  2.2 0.9 copy-start.1

commit v7 on v5

--- a/solution.py
+++ b/solution.py
@@ -446,15 +446,23 @@
     arrived(gr_recv, 7)
     back = gr_recv[...].astype(jnp.float32).reshape(slots, unit).astype(jnp.bfloat16)
     picked = dot(table[...], back, 0, 0)
+    row = lax.broadcasted_iota(jnp.int32, (count, 2 * count), 0)
+    column = lax.broadcasted_iota(jnp.int32, (count, 2 * count), 1)
+    wanted = 4 * lax.rem(row, tok) + 2 * (row // tok)
+    rows = [[], []]
     for choice in range(2):
         gate, up = gate_and_up(choice)
         sig = jax.nn.sigmoid(gate)
         grad_hidden = picked[choice * tok : (choice + 1) * tok]
-        at = choice * 2 * unit
-        ggu_ref[:, at : at + unit] = (
-            grad_hidden * up * sig * (1.0 + gate * (1.0 - sig))
-        ).astype(jnp.bfloat16)
-        ggu_ref[:, at + unit : at + 2 * unit] = (grad_hidden * (gate * sig)).astype(jnp.bfloat16)
+        rows[0].append(
+            (grad_hidden * up * sig * (1.0 + gate * (1.0 - sig))).astype(jnp.bfloat16)
+        )
+        rows[1].append((grad_hidden * (gate * sig)).astype(jnp.bfloat16))
+    spread = [
+        dot((column == wanted + kind).astype(jnp.bfloat16), jnp.concatenate(rows[kind], axis=0), 0, 0)
+        for kind in range(2)
+    ]
+    ggu_ref[...] = (spread[0] + spread[1]).astype(jnp.bfloat16)
     for src, at in unsent:
         sent(src, at)
     chips_sent(g_recv, GRADS)
@@ -466,6 +474,17 @@
     def _():
         for part in range(PARTS):
             sent(u_out.at[part, pl.ds(0, places - 1)], 8 + PARTS)
+
+
+def hand_out(*refs):
+    sources, targets, sem = refs[:3], refs[3:6], refs[6]
+    copies = [
+        pltpu.make_async_copy(sources[at], targets[at], sem.at[at]) for at in (2, 0, 1)
+    ]
+    for copy in copies:
+        copy.start()
+    for copy in copies:
+        copy.wait()
 
 
 def local(
@@ -519,7 +538,7 @@
         functools.partial(kernel, places, n_hidden, capacity),
         out_shape=(
             jax.ShapeDtypeStruct((feat, tok), bf16),
-            jax.ShapeDtypeStruct((tok, top * 2 * unit), bf16),
+            jax.ShapeDtypeStruct((tok * top * 2, unit), bf16),
             jax.ShapeDtypeStruct((unit, depth), bf16),
         ),
         in_specs=[vmem] * 5 + [anywhere] * 3,
@@ -544,6 +563,15 @@
         first_moment[0],
         second_moment[0],
     )
+    results = (combined, grads, update)
+    combined, grads, update = pl.pallas_call(
+        hand_out,
+        out_shape=tuple(jax.ShapeDtypeStruct(out.shape, out.dtype) for out in results),
+        in_specs=[anywhere] * 3,
+        out_specs=(anywhere,) * 3,
+        scratch_shapes=[pltpu.SemaphoreType.DMA((3,))],
+        compiler_params=pltpu.CompilerParams(vmem_limit_bytes=VMEM_BYTES),
+    )(*results)
     return combined.T, grads.reshape(tok, top, 2, unit), update[None]
 
 

time: 166 us -> 165 us (level)
  local copies, waits for them, and re-layouts: 3.3 us -> 1.04 us
where the time goes in v7:
time: 165 us; the launch traced here: 164 us
  Pallas kernels  162 us (98%)
    pallas_call x1, Pallas kernels, local(): pl.pallas_call(functools.partial(kernel, places, n_hidden, capacity), out...  161 us

profile of v7, /device:TPU:24, one launch (start us, length us, event | category | flops | bytes accessed | tf_op | source)
XLA Modules:
  0.0 164.1 jit_solution(12043728515043923650)
XLA Ops:
  0.6 0.0 copy-start
  0.6 0.0 copy-start.1
  0.7 0.0 copy-start.2
  0.7 0.0 copy-start.3
  0.7 1.0 reshape.12.acts_ref
  1.7 0.0 copy-done
  1.7 0.0 copy-done.1
  1.7 0.0 copy-done.2
  1.7 0.0 copy-done.3
  1.7 161.3 %shard_map.103 = (bf16[448,128]{1,0:T(8,128)(2,1)S(1)}, bf16[512,128]{1,0:T(8,128)(2,1)S(1)}, bf16[128,3584]{1,0:T(8,128)(2,1)S(1)}) custom-call(s32[2,32]{1,0:T(2,128)S(1)} %bitcast.11, s32[2,128]{1,0:T(2,128)S(1)} %bitcast.12, f32[2,128]{1,0:T(2,128)S(1)} %bitcast.13, bf16[128,512]{1,0:T(8,128)(2,1)S(1)} %reshape.12.acts_ref, ...), custom_call_target="tpu_custom_call" | custom-call | tf_op jit(solution)/shard_map/pallas_call | solution.py:537
  163.0 1.0 shard_map.104
Async XLA Ops:
  0.6 1.1 copy-start
  0.6 1.1 copy-start.1
  0.7 1.1 copy-start.2
  0.7 1.1 copy-start.3

commit v8 on v7

--- a/solution.py
+++ b/solution.py
@@ -80,6 +80,8 @@
     row_groups = m_here.shape[0] // ROWS
     col_groups = m_here.shape[1] // COLS
     stride = places // row_groups
+    halves = 2 if row_groups % 2 == 0 else 1
+    half_rows = m_here.shape[0] // halves
 
     def far_first(at, step, length):
         near = length - step
@@ -321,10 +323,31 @@
     to_chips(y_send, y_recv, OUTPUTS, 1, places // 4)
     from_chips(g_recv, g_rows, GRADS)
     grads = g_rows[...]
-    send_blocks(lambda block: dot(h_all[block], grads, 0, 0), gw_send, gw_recv, 5)
+    for half in range(halves):
+        part = pl.ds(half * half_rows, half_rows)
+
+        def send_half(step, carry, half=half, part=part):
+            peer = hidden_peer(step)
+            if half == 0:
+                gw_send[peer] = dot(h_all[peer], grads, 0, 0).astype(jnp.bfloat16)
+            pltpu.make_async_remote_copy(
+                src_ref=gw_send.at[peer, part],
+                dst_ref=gw_recv.at[mine, part],
+                send_sem=send_sem.at[10 + half],
+                recv_sem=recv_sem.at[10 + half],
+                device_id={"hidden": peer},
+            ).start()
+            return carry
+
+        lax.fori_loop(1, n_hidden, send_half, 0)
+        if half == 0:
+            gw_send[mine] = dot(h_all[mine], grads, 0, 0).astype(jnp.bfloat16)
+        pltpu.make_async_copy(
+            gw_send.at[mine, part], gw_recv.at[mine, part], recv_sem.at[10 + half]
+        ).start()
+        unsent.append((gw_recv.at[pl.ds(0, n_hidden - 1), part], 10 + half))
     to_chips(y_send, y_recv, OUTPUTS, places // 4, places // 2)
 
-    arrived(gw_recv, 5)
     for load in loads:
         load.wait()
 
@@ -336,7 +359,13 @@
 
     my_group, my_seat = me // stride, lax.rem(me, stride)
     is_mid = my_seat != spare_seat(my_group)
-    my_row = pl.multiple_of(my_group * ROWS, ROWS)
+
+    def rows_of(group):
+        per_half = row_groups // halves
+        seat = lax.rem(group, halves) * per_half + group // halves
+        return pl.multiple_of(seat * ROWS, ROWS)
+
+    my_row = rows_of(my_group)
     my_col = (my_seat - past_spare(my_seat, my_group)) * COLS
     wide = COLS // PARTS
 
@@ -344,7 +373,7 @@
         return pl.ds(pl.multiple_of(base + part * wide, wide), wide)
 
     def send_rows(group, part):
-        at = pl.multiple_of(group * ROWS, ROWS)
+        at = rows_of(group)
 
         def send(col, carry):
             peer = group * stride + col + past_spare(col, group)
@@ -368,12 +397,9 @@
 
         lax.fori_loop(0, col_groups, send, 0)
 
-    def row_group(step):
-        return far_first(me // stride, step, row_groups)
-
-    def update_rows(step, carry):
-        group = row_group(step)
-        at = pl.multiple_of(group * ROWS, ROWS)
+    def update_rows(step, carry, half):
+        group = halves * far_first(my_group // halves, step, row_groups // halves) + half
+        at = rows_of(group)
         for pair in range(n_hidden // 2):
             span = slice(pair * 2 * feat, (pair + 1) * 2 * feat)
             grad = jnp.concatenate(
@@ -393,7 +419,11 @@
         send_rows(group, 0)
         return carry
 
-    lax.fori_loop(1, row_groups + 1, update_rows, 0)
+    for half in range(halves):
+        arrived(gw_recv.at[:, pl.ds(half * half_rows, half_rows)], 10 + half)
+        lax.fori_loop(
+            1, row_groups // halves + 1, functools.partial(update_rows, half=half), 0
+        )
     send_blocks(lambda block: dot(grads, w_all[block], 1, 1), gh_send, gh_recv, 6)
 
     from_chips(y_recv, y_rows, OUTPUTS)

time: 165 us -> 164 us (level)
  no operation moved by 1% of the time
where the time goes in v8:
time: 164 us
  Pallas kernels  163 us (99%)
    pallas_call x1, Pallas kernels, local(): pl.pallas_call(functools.partial(kernel, places, n_hidden, capacity), out...  162 us

profile of v8, /device:TPU:24, one launch (start us, length us, event | category | flops | bytes accessed | tf_op | source)
XLA Modules:
  0.0 164.3 jit_solution(3710786411839662667)
XLA Ops:
  0.6 0.0 copy-start
  0.6 0.0 copy-start.1
  0.7 0.0 copy-start.2
  0.7 0.0 copy-start.3
  0.7 1.0 reshape.12.acts_ref
  1.7 0.0 copy-done
  1.7 0.0 copy-done.1
  1.7 0.0 copy-done.2
  1.7 0.0 copy-done.3
  1.7 161.5 %shard_map.103 = (bf16[448,128]{1,0:T(8,128)(2,1)S(1)}, bf16[512,128]{1,0:T(8,128)(2,1)S(1)}, bf16[128,3584]{1,0:T(8,128)(2,1)S(1)}) custom-call(s32[2,32]{1,0:T(2,128)S(1)} %bitcast.11, s32[2,128]{1,0:T(2,128)S(1)} %bitcast.12, f32[2,128]{1,0:T(2,128)S(1)} %bitcast.13, bf16[128,512]{1,0:T(8,128)(2,1)S(1)} %reshape.12.acts_ref, ...), custom_call_target="tpu_custom_call" | custom-call | tf_op jit(solution)/shard_map/pallas_call | solution.py:567
  163.3 1.0 shard_map.104
Async XLA Ops:
  0.6 1.1 copy-start
  0.6 1.1 copy-start.1
  0.7 1.1 copy-start.2
  0.7 1.1 copy-start.3
